TPU v7x, 128 devices: a whole 4x4x4 slice. The times are simulated.
128 devices in a mesh: wide: 32 (over y, z, core), narrow: 4 (over x).
Axes of the slice: x: 4, y: 4, z: 4, core: 2. Of those that a mesh axis runs over, the one named last changes fastest.
Arguments:
- prefit_resid: float32 [5242880], P(('wide', 'narrow')), may hold values from -6 to 6
- source_partials: float32 [5, 5242880], P(None, ('wide', 'narrow')), may hold values from -6 to 6
- attitude_partials: float32 [4, 5242880], P(None, ('wide', 'narrow')), may hold values from -0.25 to 0.25
- spline_position: float32 [5242880], P(('wide', 'narrow')), may hold values from 0 to 1
- calib_partials: float32 [3, 5242880], P(None, ('wide', 'narrow')), may hold values from -2 to 2
- obs_source: int32 [5242880], P(('wide', 'narrow')), may hold values from 0 to 127
- block_count: int32 [8192], P(('wide', 'narrow')), may hold values from 320 to 640, as said below
- obs_range: int32 [5242880], P(('wide', 'narrow')), may hold values from 0 to 31, as said below
- obs_knot: int32 [5242880], P(('wide', 'narrow')), may hold values from 0 to 255
- obs_unit: int32 [5242880], P(('wide', 'narrow')), may hold values from 0 to 2015
- given_inverse: float32 [32, 1024, 1024], P('wide'), may hold values from -2.5 to 2.5, as said below
- knot_decay: float32 [4, 8192], P(None, 'wide'), may hold values from 0.15 to 1
Outputs:
- source_update: float32 [5, 1048576], P(None, ('wide', 'narrow'))
- attitude_update: float32 [4, 8192], P(None, 'wide')
- cal_update: float32 [3, 2016], P(None, 'narrow')
Inputs may be any that keep to these rules, and one draw needn't show every extreme that they name: `block_count`: each block's live observations are its first slots; every device has one block with all 640 slots live. `obs_range`: at most 2560 of one device's observation slots fall in one time range; for each index along narrow, some time range holds exactly 2560 slots of every device of that index. `given_inverse`: each time range's given inverse is symmetric.
All inputs are finite; a program needn't handle non-finite values.
Results may differ from a plain program's by a relative error of at most 0.0003.
Values sent between devices are 32-bit elements; how exact they have to be, the bound alone decides.
No kernel may reach another device: no remote copies, remote signals or barrier semaphores. Data moves between devices by JAX's collectives and lax.ppermute only.
A program may use at most 64 MiB of HBM per device.

v0:
```python
import math

import jax
import jax.numpy as jnp
from jax import lax
from jax.sharding import PartitionSpec as P

SRC_BLK = 128
SLOT_BLK = 640
CAL = 2016


source_pairs = [(left_at, right_at) for left_at in range(5) for right_at in range(left_at, 5)]
calib_pairs = [(left_at, right_at) for left_at in range(3) for right_at in range(left_at, 3)]


def entering_2(value, axis, join, neutral):
    count, mine = (lax.axis_size(axis), lax.axis_index(axis))
    pieces = jax.tree.map(lambda part: lax.all_gather(part, axis), value)
    running = jax.tree.map(
        lambda part, zero: jnp.full_like(part, 0) + jnp.asarray(zero, part.dtype), value, neutral
    )

    def step(position, running):
        longer = join(running, jax.tree.map(lambda part: part[position], pieces))
        return jax.tree.map(lambda new, old: jnp.where(position < mine, new, old), longer, running)

    return lax.fori_loop(0, count - 1, step, running)


def spline(position):
    remain = 1.0 - position
    square_pos = position * position
    cube_pos = square_pos * position
    return jnp.stack(
        [
            remain * remain * remain / 6.0,
            (3.0 * cube_pos - 6.0 * square_pos + 4.0) / 6.0,
            (-3.0 * cube_pos + 3.0 * square_pos + 3.0 * position + 1.0) / 6.0,
            cube_pos / 6.0,
        ]
    )


def symmetric(values, pair_list, order_size):
    matrix = [[None] * order_size for index_lookup in range(order_size)]
    for slot_at, (left_at, right_at) in enumerate(pair_list):
        diag_add = 1.0 if left_at == right_at else 0.0
        entry_val = values[slot_at] + diag_add
        matrix[left_at][right_at] = entry_val
        matrix[right_at][left_at] = entry_val
    return matrix


def spd_solve(matrix, target):
    order_size = len(target)
    lower_tri = [[None] * order_size for index_lookup in range(order_size)]
    for column in range(order_size):
        pivot_sq = matrix[column][column]
        for before in range(column):
            pivot_sq = pivot_sq - lower_tri[column][before] * lower_tri[column][before]
        pivot_root = jnp.sqrt(pivot_sq)
        lower_tri[column][column] = pivot_root
        for row_at in range(column + 1, order_size):
            entry_val = matrix[row_at][column]
            for before in range(column):
                entry_val = entry_val - lower_tri[row_at][before] * lower_tri[column][before]
            lower_tri[row_at][column] = entry_val / pivot_root
    forward_sol = []
    for row_at in range(order_size):
        running = target[row_at]
        for before in range(row_at):
            running = running - lower_tri[row_at][before] * forward_sol[before]
        forward_sol.append(running / lower_tri[row_at][row_at])
    answer = [None] * order_size
    for row_at in reversed(range(order_size)):
        running = forward_sol[row_at]
        for before in range(row_at + 1, order_size):
            running = running - lower_tri[before][row_at] * answer[before]
        answer[row_at] = running / lower_tri[row_at][row_at]
    return answer


def chain_step(earlier, later):
    return (earlier[0] * later[0], later[0] * earlier[1] + later[1])


def pair_sum(values, first_ids, first_count, second_ids, second_count):
    row_count = values.shape[0]
    slot_count = values.shape[1]
    piece_size = math.gcd(slot_count, 2048)
    turn_count = slot_count // piece_size
    first_grid = jnp.arange(first_count, dtype=jnp.int32)
    second_grid = jnp.arange(second_count, dtype=jnp.int32)

    def accumulate(turn_at, running):
        starting_offset = turn_at * piece_size
        value_piece = lax.dynamic_slice_in_dim(values, starting_offset, piece_size, 1)
        first_piece = lax.dynamic_slice_in_dim(first_ids, starting_offset, piece_size, 0)
        second_piece = lax.dynamic_slice_in_dim(second_ids, starting_offset, piece_size, 0)
        first_hot = (first_grid[:, None] == first_piece[None, :]).astype(jnp.float32)
        left_rows = (value_piece[:, None, :] * first_hot[None, :, :]).reshape(
            row_count * first_count, piece_size
        )
        second_hot = (second_piece[:, None] == second_grid[None, :]).astype(jnp.float32)
        return running + jnp.dot(left_rows, second_hot, precision=lax.Precision.HIGHEST)

    totals = lax.fori_loop(
        0, turn_count, accumulate, jnp.zeros((row_count * first_count, second_count), jnp.float32)
    )
    return totals.reshape(row_count, first_count, second_count)


def shifted_knots(totals, knot_count):
    result = jnp.zeros((4, knot_count + 3), jnp.float32)
    for shift_at in range(4):
        result = result + jnp.pad(totals[shift_at], ((0, 0), (shift_at, 3 - shift_at)))
    return result


def on_device(
    prefit_resid,
    source_partials,
    attitude_partials,
    spline_position,
    calib_partials,
    obs_source,
    block_count,
    obs_range,
    obs_knot,
    obs_unit,
    given_inverse,
    knot_decay,
):
    ranges = lax.axis_size("wide")
    groups = lax.axis_size("narrow")
    blocks = block_count.shape[0]
    count_obs = prefit_resid.shape[0]
    knots_dev = knot_decay.shape[1]
    valid_grid = (jnp.arange(SLOT_BLK, dtype=jnp.int32)[None, :] < block_count[:, None]).astype(
        jnp.float32
    )
    valid_mask = valid_grid.reshape(count_obs)
    member = (
        obs_source.reshape(blocks, SLOT_BLK)[:, :, None]
        == jnp.arange(SRC_BLK, dtype=jnp.int32)[None, None, :]
    ).astype(jnp.float32) * valid_grid[:, :, None]
    quantities = [
        source_partials[left_at] * source_partials[right_at] for left_at, right_at in source_pairs
    ]
    quantities = quantities + [source_partials[param_at] * prefit_resid for param_at in range(5)]
    stacked = jnp.stack(quantities).reshape(20, blocks, SLOT_BLK)
    block_sums = jnp.einsum(
        "qbs,bsk->qbk", stacked, member, precision=lax.Precision.HIGHEST
    ).reshape(20, blocks * SRC_BLK)
    matrix = symmetric([block_sums[index_lookup] for index_lookup in range(15)], source_pairs, 5)
    source_update = jnp.stack(
        spd_solve(matrix, [block_sums[15 + param_at] for param_at in range(5)])
    )
    update_at_obs = jnp.einsum(
        "pbk,bsk->pbs",
        source_update.reshape(5, blocks, SRC_BLK),
        member,
        precision=lax.Precision.HIGHEST,
    ).reshape(5, count_obs)
    resid_after = valid_mask * (prefit_resid - jnp.sum(source_partials * update_at_obs, axis=0))
    masked_cal = valid_mask * calib_partials
    cal_terms = [masked_cal[left_at] * masked_cal[right_at] for left_at, right_at in calib_pairs]
    cal_terms = cal_terms + [masked_cal[param_at] * resid_after for param_at in range(3)]
    no_range = jnp.zeros((count_obs,), jnp.int32)
    cal_partial = pair_sum(jnp.stack(cal_terms), no_range, 1, obs_unit, CAL).reshape(9, CAL)
    cal_summed = lax.psum(cal_partial, ("wide", "narrow"))
    share_size = CAL // groups
    cal_mine = lax.dynamic_slice_in_dim(
        cal_summed, lax.axis_index("narrow") * share_size, share_size, 1
    )
    cal_matrix = symmetric([cal_mine[index_lookup] for index_lookup in range(6)], calib_pairs, 3)
    cal_update = jnp.stack(spd_solve(cal_matrix, [cal_mine[6 + param_at] for param_at in range(3)]))
    weights = spline(spline_position)
    total_knots = knots_dev * ranges
    term_rows = (
        weights[:, None, :] * attitude_partials[None, :, :] * resid_after[None, None, :]
    ).reshape(16, count_obs)
    totals = pair_sum(term_rows, obs_range, ranges, obs_knot, knots_dev).reshape(4, 4, total_knots)
    partial_rhs = shifted_knots(totals, total_knots)[:, :total_knots]
    own_rhs = lax.psum(
        lax.psum_scatter(partial_rhs, "wide", scatter_dimension=1, tiled=True), "narrow"
    )
    solution_vector = jnp.dot(
        given_inverse[0], own_rhs.reshape(4 * knots_dev), precision=lax.Precision.HIGHEST
    ).reshape(4, knots_dev)
    knot_gain = jnp.sqrt(1.0 - knot_decay * knot_decay)
    carry_mul, carry_add = lax.associative_scan(
        chain_step, (knot_decay, knot_gain * solution_vector), axis=1
    )
    entering = entering_2(
        (carry_mul[:, -1], carry_add[:, -1]),
        "wide",
        chain_step,
        (jnp.ones((4,), jnp.float32), jnp.zeros((4,), jnp.float32)),
    )
    attitude_update = carry_add + carry_mul * entering[1][:, None]
    return (source_update, attitude_update, cal_update)


def solution(mesh):
    placed = (
        P(("wide", "narrow")),
        P(None, ("wide", "narrow")),
        P(None, ("wide", "narrow")),
        P(("wide", "narrow")),
        P(None, ("wide", "narrow")),
        P(("wide", "narrow")),
        P(("wide", "narrow")),
        P(("wide", "narrow")),
        P(("wide", "narrow")),
        P(("wide", "narrow")),
        P("wide", None, None),
        P(None, "wide"),
    )
    return jax.shard_map(
        on_device,
        mesh=mesh,
        in_specs=placed,
        out_specs=(P(None, ("wide", "narrow")), P(None, "wide"), P(None, "narrow")),
        check_vma=False,
    )
```

profile of v0, /device:TPU:1, one launch (start us, length us, event | category | flops | bytes accessed | tf_op | source)
XLA Modules:
  0.0 645.8 jit_solution(9683964200832528434)
XLA Ops:
  8.1 6.3 fusion.52
  14.4 4.9 fusion.53
  20.9 12.2 %stack.132 = f32[20,64,640]{2,0,1:T(8,128)} concatenate(f32[1,64,640]{2,0,1:T(1,128)S(1)} %bitcast.134, f32[1,64,640]{2,0,1:T(1,128)S(1)} %bitcast.135, f32[1,64,640]{2,0,1:T(1,128)S(1)} %bitcast.137, f32[1,64,640]{2,0,1:T(1,128)} %bitcast.140, f32[1,64,640]{2,0,1:T(1,128)} %bitcast.144, f32[1,64,640]{2,0,1:T(1,128)S(1)} %bitcast.136, f32[1,64,640]{2,0,1:T(1,128)S(1)} %bitcast.138, ...), dimensions={0} | concatenate | bytes 6553600 | tf_op jit(solution)/shard_map/stack | solution.py:152
  33.1 26.6 %fusion.17 = f32[64,128,20]{1,2,0:T(8,128)S(1)} fusion(f32[20,64,640]{2,0,1:T(8,128)} %stack.132, f32[64,640]{1,0:T(8,128)S(1)} %copy-done.5, s32[64,640]{1,0:T(8,128)S(1)} %copy-done.6), kind=kOutput, calls=%fused_computation.23 | convolution fusion | flops 1268776960 | bytes 4259840 | tf_op jit(solution)/shard_map/qbs,bsk->qbk/dot_general | solution.py:153
  61.6 38.2 %fusion.15 = f32[64,640,5]{1,2,0:T(8,128)S(1)} fusion(f32[64,640]{1,0:T(8,128)S(1)} %copy-done.5, s32[64,640]{1,0:T(8,128)S(1)} %copy-done.7, f32[5,64,128]{2,1,0:T(8,128)S(1)} %constant_dynamic-update-slice_fusion), kind=kOutput, calls=%fused_computation.21 | convolution fusion | flops 325058560 | bytes 1310720 | tf_op jit(solution)/shard_map/pbk,bsk->pbs/dot_general | solution.py:160
  106.5 151.7 %while.44 = (s32[]{:T(128)}, f32[9,2016]{1,0:T(8,128)}, f32[9,40960]{1,0:T(8,128)S(1)}, s32[40960]{0:T(1024)}, s32[]{:T(128)}, /*index=5*/s32[]{:T(128)}, s32[]{:T(128)}, s32[]{:T(128)}) while((s32[]{:T(128)}, f32[9,2016]{1,0:T(8,128)}, f32[9,40960]{1,0:T(8,128)S(1)}, s32[40960]{0:T(1024)}, s32[]{:T(128)}, /*index=5*/s32[]{:T(128)}, ...), condition=%wide.region_8.9_spmd.clone, body=%wide.region_7.8_spmd.clone.sunk | while | flops 450072000 | bytes 300949 | solution.py:108
  107.3 6.0 fusion.80
  114.0 6.9 %fusion.80 = f32[9,2016]{1,0:T(8,128)} fusion(s32[2048]{0:T(1024)S(1)} %dynamic_slice.78, f32[9,2016]{1,0:T(8,128)} %get-tuple-element.702, f32[9,40960]{1,0:T(8,128)S(1)} %get-tuple-element.711, s32[]{:T(128)S(6)} %select_n.56, pred[]{:T(512)S(6)} %compare.47), kind=kOutput, calls=%fused_computation.18.clone.1 | convolution fusion | flops 450072000 | bytes 284421 | tf_op jit(solution)/shard_map/while/body/eval_jaxpr/dot_general | solution.py:106
  121.6 6.9 %fusion.80 = f32[9,2016]{1,0:T(8,128)} fusion(s32[2048]{0:T(1024)S(1)} %dynamic_slice.78, f32[9,2016]{1,0:T(8,128)} %get-tuple-element.702, f32[9,40960]{1,0:T(8,128)S(1)} %get-tuple-element.711, s32[]{:T(128)S(6)} %select_n.56, pred[]{:T(512)S(6)} %compare.47), kind=kOutput, calls=%fused_computation.18.clone.1 | convolution fusion | flops 450072000 | bytes 284421 | tf_op jit(solution)/shard_map/while/body/eval_jaxpr/dot_general | solution.py:106
  129.3 6.9 %fusion.80 = f32[9,2016]{1,0:T(8,128)} fusion(s32[2048]{0:T(1024)S(1)} %dynamic_slice.78, f32[9,2016]{1,0:T(8,128)} %get-tuple-element.702, f32[9,40960]{1,0:T(8,128)S(1)} %get-tuple-element.711, s32[]{:T(128)S(6)} %select_n.56, pred[]{:T(512)S(6)} %compare.47), kind=kOutput, calls=%fused_computation.18.clone.1 | convolution fusion | flops 450072000 | bytes 284421 | tf_op jit(solution)/shard_map/while/body/eval_jaxpr/dot_general | solution.py:106
  136.9 6.9 %fusion.80 = f32[9,2016]{1,0:T(8,128)} fusion(s32[2048]{0:T(1024)S(1)} %dynamic_slice.78, f32[9,2016]{1,0:T(8,128)} %get-tuple-element.702, f32[9,40960]{1,0:T(8,128)S(1)} %get-tuple-element.711, s32[]{:T(128)S(6)} %select_n.56, pred[]{:T(512)S(6)} %compare.47), kind=kOutput, calls=%fused_computation.18.clone.1 | convolution fusion | flops 450072000 | bytes 284421 | tf_op jit(solution)/shard_map/while/body/eval_jaxpr/dot_general | solution.py:106
  144.5 6.9 %fusion.80 = f32[9,2016]{1,0:T(8,128)} fusion(s32[2048]{0:T(1024)S(1)} %dynamic_slice.78, f32[9,2016]{1,0:T(8,128)} %get-tuple-element.702, f32[9,40960]{1,0:T(8,128)S(1)} %get-tuple-element.711, s32[]{:T(128)S(6)} %select_n.56, pred[]{:T(512)S(6)} %compare.47), kind=kOutput, calls=%fused_computation.18.clone.1 | convolution fusion | flops 450072000 | bytes 284421 | tf_op jit(solution)/shard_map/while/body/eval_jaxpr/dot_general | solution.py:106
  152.1 6.9 %fusion.80 = f32[9,2016]{1,0:T(8,128)} fusion(s32[2048]{0:T(1024)S(1)} %dynamic_slice.78, f32[9,2016]{1,0:T(8,128)} %get-tuple-element.702, f32[9,40960]{1,0:T(8,128)S(1)} %get-tuple-element.711, s32[]{:T(128)S(6)} %select_n.56, pred[]{:T(512)S(6)} %compare.47), kind=kOutput, calls=%fused_computation.18.clone.1 | convolution fusion | flops 450072000 | bytes 284421 | tf_op jit(solution)/shard_map/while/body/eval_jaxpr/dot_general | solution.py:106
  159.8 6.9 %fusion.80 = f32[9,2016]{1,0:T(8,128)} fusion(s32[2048]{0:T(1024)S(1)} %dynamic_slice.78, f32[9,2016]{1,0:T(8,128)} %get-tuple-element.702, f32[9,40960]{1,0:T(8,128)S(1)} %get-tuple-element.711, s32[]{:T(128)S(6)} %select_n.56, pred[]{:T(512)S(6)} %compare.47), kind=kOutput, calls=%fused_computation.18.clone.1 | convolution fusion | flops 450072000 | bytes 284421 | tf_op jit(solution)/shard_map/while/body/eval_jaxpr/dot_general | solution.py:106
  167.4 6.9 %fusion.80 = f32[9,2016]{1,0:T(8,128)} fusion(s32[2048]{0:T(1024)S(1)} %dynamic_slice.78, f32[9,2016]{1,0:T(8,128)} %get-tuple-element.702, f32[9,40960]{1,0:T(8,128)S(1)} %get-tuple-element.711, s32[]{:T(128)S(6)} %select_n.56, pred[]{:T(512)S(6)} %compare.47), kind=kOutput, calls=%fused_computation.18.clone.1 | convolution fusion | flops 450072000 | bytes 284421 | tf_op jit(solution)/shard_map/while/body/eval_jaxpr/dot_general | solution.py:106
  175.0 6.9 %fusion.80 = f32[9,2016]{1,0:T(8,128)} fusion(s32[2048]{0:T(1024)S(1)} %dynamic_slice.78, f32[9,2016]{1,0:T(8,128)} %get-tuple-element.702, f32[9,40960]{1,0:T(8,128)S(1)} %get-tuple-element.711, s32[]{:T(128)S(6)} %select_n.56, pred[]{:T(512)S(6)} %compare.47), kind=kOutput, calls=%fused_computation.18.clone.1 | convolution fusion | flops 450072000 | bytes 284421 | tf_op jit(solution)/shard_map/while/body/eval_jaxpr/dot_general | solution.py:106
  182.6 6.9 %fusion.80 = f32[9,2016]{1,0:T(8,128)} fusion(s32[2048]{0:T(1024)S(1)} %dynamic_slice.78, f32[9,2016]{1,0:T(8,128)} %get-tuple-element.702, f32[9,40960]{1,0:T(8,128)S(1)} %get-tuple-element.711, s32[]{:T(128)S(6)} %select_n.56, pred[]{:T(512)S(6)} %compare.47), kind=kOutput, calls=%fused_computation.18.clone.1 | convolution fusion | flops 450072000 | bytes 284421 | tf_op jit(solution)/shard_map/while/body/eval_jaxpr/dot_general | solution.py:106
  190.3 6.9 %fusion.80 = f32[9,2016]{1,0:T(8,128)} fusion(s32[2048]{0:T(1024)S(1)} %dynamic_slice.78, f32[9,2016]{1,0:T(8,128)} %get-tuple-element.702, f32[9,40960]{1,0:T(8,128)S(1)} %get-tuple-element.711, s32[]{:T(128)S(6)} %select_n.56, pred[]{:T(512)S(6)} %compare.47), kind=kOutput, calls=%fused_computation.18.clone.1 | convolution fusion | flops 450072000 | bytes 284421 | tf_op jit(solution)/shard_map/while/body/eval_jaxpr/dot_general | solution.py:106
  197.9 6.9 %fusion.80 = f32[9,2016]{1,0:T(8,128)} fusion(s32[2048]{0:T(1024)S(1)} %dynamic_slice.78, f32[9,2016]{1,0:T(8,128)} %get-tuple-element.702, f32[9,40960]{1,0:T(8,128)S(1)} %get-tuple-element.711, s32[]{:T(128)S(6)} %select_n.56, pred[]{:T(512)S(6)} %compare.47), kind=kOutput, calls=%fused_computation.18.clone.1 | convolution fusion | flops 450072000 | bytes 284421 | tf_op jit(solution)/shard_map/while/body/eval_jaxpr/dot_general | solution.py:106
  205.5 6.9 %fusion.80 = f32[9,2016]{1,0:T(8,128)} fusion(s32[2048]{0:T(1024)S(1)} %dynamic_slice.78, f32[9,2016]{1,0:T(8,128)} %get-tuple-element.702, f32[9,40960]{1,0:T(8,128)S(1)} %get-tuple-element.711, s32[]{:T(128)S(6)} %select_n.56, pred[]{:T(512)S(6)} %compare.47), kind=kOutput, calls=%fused_computation.18.clone.1 | convolution fusion | flops 450072000 | bytes 284421 | tf_op jit(solution)/shard_map/while/body/eval_jaxpr/dot_general | solution.py:106
  213.2 6.9 %fusion.80 = f32[9,2016]{1,0:T(8,128)} fusion(s32[2048]{0:T(1024)S(1)} %dynamic_slice.78, f32[9,2016]{1,0:T(8,128)} %get-tuple-element.702, f32[9,40960]{1,0:T(8,128)S(1)} %get-tuple-element.711, s32[]{:T(128)S(6)} %select_n.56, pred[]{:T(512)S(6)} %compare.47), kind=kOutput, calls=%fused_computation.18.clone.1 | convolution fusion | flops 450072000 | bytes 284421 | tf_op jit(solution)/shard_map/while/body/eval_jaxpr/dot_general | solution.py:106
  220.8 6.9 %fusion.80 = f32[9,2016]{1,0:T(8,128)} fusion(s32[2048]{0:T(1024)S(1)} %dynamic_slice.78, f32[9,2016]{1,0:T(8,128)} %get-tuple-element.702, f32[9,40960]{1,0:T(8,128)S(1)} %get-tuple-element.711, s32[]{:T(128)S(6)} %select_n.56, pred[]{:T(512)S(6)} %compare.47), kind=kOutput, calls=%fused_computation.18.clone.1 | convolution fusion | flops 450072000 | bytes 284421 | tf_op jit(solution)/shard_map/while/body/eval_jaxpr/dot_general | solution.py:106
  228.4 6.9 %fusion.80 = f32[9,2016]{1,0:T(8,128)} fusion(s32[2048]{0:T(1024)S(1)} %dynamic_slice.78, f32[9,2016]{1,0:T(8,128)} %get-tuple-element.702, f32[9,40960]{1,0:T(8,128)S(1)} %get-tuple-element.711, s32[]{:T(128)S(6)} %select_n.56, pred[]{:T(512)S(6)} %compare.47), kind=kOutput, calls=%fused_computation.18.clone.1 | convolution fusion | flops 450072000 | bytes 284421 | tf_op jit(solution)/shard_map/while/body/eval_jaxpr/dot_general | solution.py:106
  236.0 6.9 %fusion.80 = f32[9,2016]{1,0:T(8,128)} fusion(s32[2048]{0:T(1024)S(1)} %dynamic_slice.78, f32[9,2016]{1,0:T(8,128)} %get-tuple-element.702, f32[9,40960]{1,0:T(8,128)S(1)} %get-tuple-element.711, s32[]{:T(128)S(6)} %select_n.56, pred[]{:T(512)S(6)} %compare.47), kind=kOutput, calls=%fused_computation.18.clone.1 | convolution fusion | flops 450072000 | bytes 284421 | tf_op jit(solution)/shard_map/while/body/eval_jaxpr/dot_general | solution.py:106
  243.7 6.9 %fusion.80 = f32[9,2016]{1,0:T(8,128)} fusion(s32[2048]{0:T(1024)S(1)} %dynamic_slice.78, f32[9,2016]{1,0:T(8,128)} %get-tuple-element.702, f32[9,40960]{1,0:T(8,128)S(1)} %get-tuple-element.711, s32[]{:T(128)S(6)} %select_n.56, pred[]{:T(512)S(6)} %compare.47), kind=kOutput, calls=%fused_computation.18.clone.1 | convolution fusion | flops 450072000 | bytes 284421 | tf_op jit(solution)/shard_map/while/body/eval_jaxpr/dot_general | solution.py:106
  251.3 6.9 %fusion.80 = f32[9,2016]{1,0:T(8,128)} fusion(s32[2048]{0:T(1024)S(1)} %dynamic_slice.78, f32[9,2016]{1,0:T(8,128)} %get-tuple-element.702, f32[9,40960]{1,0:T(8,128)S(1)} %get-tuple-element.711, s32[]{:T(128)S(6)} %select_n.56, pred[]{:T(512)S(6)} %compare.47), kind=kOutput, calls=%fused_computation.18.clone.1 | convolution fusion | flops 450072000 | bytes 284421 | tf_op jit(solution)/shard_map/while/body/eval_jaxpr/dot_general | solution.py:106
  266.4 190.7 %while.42 = (s32[]{:T(128)}, f32[512,256]{1,0:T(8,128)S(1)}, f32[16,40960]{1,0:T(8,128)}, s32[40960]{0:T(1024)}, s32[40960]{0:T(1024)}, /*index=5*/s32[]{:T(128)}, s32[]{:T(128)}, s32[]{:T(128)}, s32[]{:T(128)}) while((s32[]{:T(128)}, f32[512,256]{1,0:T(8,128)S(1)}, f32[16,40960]{1,0:T(8,128)}, s32[40960]{0:T(1024)}, ...), condition=%wide.region_2.0_spmd.clone, body=%wide.region_1.0_spmd.clone.sunk | while | flops 3223191552 | bytes 10404001 | solution.py:108
  271.2 4.7 fusion.78
  280.7 4.7 fusion.78
  290.3 4.7 fusion.78
  299.8 4.7 fusion.78
  309.3 4.7 fusion.78
  318.9 4.7 fusion.78
  328.4 4.7 fusion.78
  338.0 4.7 fusion.78
  357.1 4.7 fusion.78
  376.2 4.7 fusion.78
  385.7 4.7 fusion.78
  395.2 4.7 fusion.78
  404.8 4.7 fusion.78
  414.3 4.7 fusion.78
  423.8 4.7 fusion.78
  433.4 4.7 fusion.78
  442.9 4.7 fusion.78
  469.5 74.9 %reduce-scatter.4.cloned.1.call-done = f32[256,4]{1,0:T(8,128)} async-done(((f32[8192,4]{1,0:T(8,128)}), f32[256,4]{1,0:T(8,128)}) %reduce-scatter.4.cloned.1.call-update) | async-done | bytes 4112
  545.4 8.4 %psum.14 = f32[1024]{0:T(1024)S(1)} all-reduce(f32[1024]{0:T(1024)S(1)} %bitcast.181), channel_id=1, replica_groups=mesh['wide'=32,'narrow'=4] {'narrow'}, use_global_device_ids=true, to_apply=%region_4.0 | all-reduce | flops 1024 | bytes 8192 | tf_op jit(solution)/shard_map/psum | solution.py:186
  553.9 5.6 fusion.60
  569.8 66.3 %all-reduce.38 = (f32[128]{0:T(128)S(1)}, f32[128]{0:T(128)S(1)}) all-reduce(f32[128]{0:T(128)S(1)} %dynamic-update-slice, f32[128]{0:T(128)S(1)} %dynamic-update-slice.1), channel_id=2, replica_groups=mesh['wide'=32,'narrow'=4] {'wide'}, use_global_device_ids=true, to_apply=%add.36 | all-reduce | flops 256 | bytes 2048
  (377 shorter events, 167.6 us)
Async XLA Ops:
  8.0 11.3 %copy-start.22 = (s32[64]{0:T(128)S(1)}, s32[64]{0:T(128)}, u32[]{:S(2)}) copy-start(s32[64]{0:T(128)} %param.24) | copy-start | bytes 772
  8.0 12.1 %copy-start.4 = (s32[40960]{0:T(1024)S(1)}, s32[40960]{0:T(1024)}, u32[]{:S(2)}) copy-start(s32[40960]{0:T(1024)} %param.23) | copy-start | bytes 491524
  8.0 12.8 %copy-start.3 = (f32[40960]{0:T(1024)S(1)}, f32[40960]{0:T(1024)}, u32[]{:S(2)}) copy-start(f32[40960]{0:T(1024)} %param.18) | copy-start | bytes 491524
  8.0 457.9 %all-reduce.41.cloned.1.call-start = ((), (), s32[]{:S(2)}) async-start(), calls=%async_computation.1 | async-start | bytes 262144 | tf_op jit(solution)/shard_map/psum | solution.py:172
  20.9 12.2 %copy-start.5 = (f32[64,640]{1,0:T(8,128)S(1)}, f32[64,640]{1,0:T(8,128)}, u32[]{:S(2)}) copy-start(f32[64,640]{1,0:T(8,128)} %get-tuple-element.555) | copy-start | bytes 491524
  20.9 12.2 %copy-start.6 = (s32[64,640]{1,0:T(8,128)S(1)}, s32[64,640]{1,0:T(8,128)}, u32[]{:S(2)}) copy-start(s32[64,640]{1,0:T(8,128)} %eq.114) | copy-start | bytes 491524
  59.7 1.9 copy-start.7
  59.8 1.7 copy-start.1
  61.5 38.3 %copy-start = (f32[5,40960]{1,0:T(8,128)S(1)}, f32[5,40960]{1,0:T(8,128)}, u32[]{:S(2)}) copy-start(f32[5,40960]{1,0:T(8,128)} %param.19) | copy-start | bytes 2457604
  61.5 38.9 %copy-start.2 = (f32[3,40960]{1,0:T(4,128)S(1)}, f32[3,40960]{1,0:T(4,128)}, u32[]{:S(2)}) copy-start(f32[3,40960]{1,0:T(4,128)} %param.22) | copy-start | bytes 1474564
  106.5 152.0 %copy-start.8 = (f32[40960]{0:T(1024)S(1)}, f32[40960]{0:T(1024)}, u32[]{:S(2)}) copy-start(f32[40960]{0:T(1024)} %param.21) | copy-start | bytes 491524
  258.3 286.2 %reduce-scatter.4.cloned.1.call-start = ((), (), s32[]{:S(2)}) async-start(), calls=%async_computation.2 | async-start | bytes 4325376
  457.7 2.8 copy-start.21
  457.7 4.4 copy-start.23
  457.8 5.6 copy-start.13
  457.8 5.6 copy-start.14
  457.8 5.6 copy-start.15
  457.8 5.6 copy-start.16
  457.8 5.6 copy-start.17
  457.8 5.6 copy-start.18
  457.8 5.6 copy-start.19
  457.8 5.6 copy-start.20
  457.8 6.3 copy-start.9
  457.8 6.3 copy-start.10
  457.9 6.3 copy-start.11
  457.9 6.3 copy-start.12
  461.3 107.6 %slice-start = ((f32[4,256]{1,0:T(4,128)}), f32[4,1]{1,0:T(4,128)S(1)}, s32[]{:S(2)}) async-start(f32[4,256]{1,0:T(4,128)} %param.29), calls=%async_computation.3 | async-start | bytes 4096 | tf_op jit(solution)/shard_map/slice | solution.py:193
Sparse Core Ops, SparseCore 0:
  258.4 143.2 all-reduce.40
Sparse Core Ops, SparseCore 1:
  460.6 83.8 reduce-scatter.3
where the time goes:
time: 651 us; the launch traced here: 646 us
  matrix products  302 us (46%)
  local copies, waits for them, and re-layouts  94.4 us (15%)
  other arithmetic  81 us (12%)
  waiting for transfers between devices  75 us (12%)
  blocking collectives  74.7 us (11%)
  between operations  17 us (3%)
    dot_general x40, matrix products, accumulate(): jnp.dot(left_rows, second_hot, precision=lax.Precision.HIGHEST)  231 us
    unnamed x3, waiting for transfers between devices  75 us
    unnamed x1, blocking collectives  66.3 us
    mul x20, other arithmetic, accumulate(): value_piece[:, None, :] * first_hot[None, :, :]  49.4 us
    dot_general x1, matrix products, on_device(): jnp.einsum('pbk,bsk->pbs', source_update.reshape(5, blocks, SRC_BLK), mem...  38.2 us
    dynamic_slice x40, local copies, waits for them, and re-layouts, accumulate(): lax.dynamic_slice_in_dim(second_ids, starting_offset, piece_size, 0)  27.9 us
    dot_general x1, matrix products, on_device(): jnp.einsum('qbs,bsk->qbk', stacked, member, precision=lax.Precision.HIGHEST)  26.6 us
    dynamic_slice x20, local copies, waits for them, and re-layouts, accumulate(): lax.dynamic_slice_in_dim(values, starting_offset, piece_size, 1)  18.4 us
  transfers between devices with their start and end apart: 2, of which 1 were waited for; matrix products, arithmetic and copies ran while one was open for 32% of the time, Pallas kernels for 0%

commit v1 on v0

v1 whole, which is shorter than its diff:
```python
import jax
import jax.numpy as jnp
from jax import lax
from jax.experimental import pallas as pl
from jax.experimental.pallas import tpu as pltpu
from jax.sharding import PartitionSpec as P

SRC_BLK = 128
SLOT_BLK = 640
CAL = 2016
GRP = 8
CHUNK = 1280
LANE = 128
ATT_BASE = 125
ATT_HI = 66
CAL_BASE = 252
CAL_HI = 8
F32 = jnp.float32
BF16 = jnp.bfloat16


def rounded(value):
    return value.astype(BF16).astype(F32)


def split3(value):
    top = rounded(value)
    rest = value - top
    mid = rounded(rest)
    return top, mid, rest - mid


def spd_solve(matrix, target):
    order = len(target)
    lower = [[None] * order for _ in range(order)]
    inv = [None] * order
    for col in range(order):
        pivot = matrix[col][col]
        for k in range(col):
            pivot = pivot - lower[col][k] * lower[col][k]
        inv[col] = 1.0 / jnp.sqrt(pivot)
        for row in range(col + 1, order):
            entry = matrix[row][col]
            for k in range(col):
                entry = entry - lower[row][k] * lower[col][k]
            lower[row][col] = entry * inv[col]
    forward = []
    for row in range(order):
        running = target[row]
        for k in range(row):
            running = running - lower[row][k] * forward[k]
        forward.append(running * inv[row])
    answer = [None] * order
    for row in reversed(range(order)):
        running = forward[row]
        for k in range(row + 1, order):
            running = running - lower[k][row] * answer[k]
        answer[row] = running * inv[row]
    return answer


NT = (((1,), (1,)), ((), ()))


def obs_kernel(
    count_ref, pre_ref, par_ref, att_ref, pos_ref, cal_ref, src_ref, rng_ref, knot_ref, unit_ref,
    upd_ref, att_out, cal_out,
    tile_s, hot_s, sums_s, upd_s, resid_s, unit_s, att_a, att_b, cal_a, cal_b, att_acc, cal_acc,
):
    step = pl.program_id(0)
    row8 = lax.broadcasted_iota(jnp.int32, (8, LANE), 0)
    row16 = lax.broadcasted_iota(jnp.int32, (16, LANE), 0)

    @pl.when(step == 0)
    def _():
        att_acc[...] = jnp.zeros_like(att_acc)
        cal_acc[...] = jnp.zeros_like(cal_acc)
        tile_s[...] = jnp.zeros_like(tile_s)

    hot_rows = lax.broadcasted_iota(jnp.int32, (SRC_BLK, SLOT_BLK), 0)
    slot = lax.broadcasted_iota(jnp.int32, (1, SLOT_BLK), 1)
    tile_s[0:5, :] = par_ref[...]
    tile_s[5:6, :] = pre_ref[...]
    for g in range(GRP):
        lanes = slice(g * SLOT_BLK, (g + 1) * SLOT_BLK)
        live = slot < count_ref[step * GRP + g]
        ids = jnp.where(live, src_ref[:, lanes], -1)
        hot = jnp.where(hot_rows == ids, 1.0, 0.0).astype(BF16)
        hot_s[g] = hot
        tile = tile_s[:, lanes]
        prods = jnp.concatenate([tile * tile[p:p + 1, :] for p in range(5)], axis=0)
        stacked = jnp.concatenate(split3(prods), axis=0).astype(BF16)
        sums = lax.dot_general(stacked, hot, NT, preferred_element_type=F32)
        sums_s[:, g, :] = sums[0:40] + sums[40:80] + sums[80:120]
    matrix = [[None] * 5 for _ in range(5)]
    for i in range(5):
        for j in range(i, 5):
            entry = sums_s[i * 8 + j] + (1.0 if i == j else 0.0)
            matrix[i][j] = entry
            matrix[j][i] = entry
    answer = spd_solve(matrix, [sums_s[i * 8 + 5] for i in range(5)])
    for p in range(5):
        upd_s[p] = answer[p]
    upd_s[5] = jnp.zeros((8, LANE), F32)
    upd_s[6] = jnp.zeros((8, LANE), F32)
    upd_s[7] = jnp.zeros((8, LANE), F32)
    for g in range(GRP):
        lanes = slice(g * SLOT_BLK, (g + 1) * SLOT_BLK)
        mine = upd_s[:, g, :]
        upd_ref[:, g * SRC_BLK:(g + 1) * SRC_BLK] = mine[0:5]
        stacked = jnp.concatenate(split3(mine), axis=0).astype(BF16)
        back = jnp.dot(stacked, hot_s[g], preferred_element_type=F32)
        back = back[0:8] + back[8:16] + back[16:24]
        live = slot < count_ref[step * GRP + g]
        fitted = jnp.sum(back * tile_s[:, lanes], axis=0, keepdims=True)
        resid_s[:, lanes] = jnp.where(live, pre_ref[:, lanes] - fitted, 0.0)
        unit_s[:, lanes] = jnp.where(live, unit_ref[:, lanes], -1)

    low8 = row8 < 4
    kk = jnp.bitwise_and(row8, 3)
    c0 = jnp.where(kk == 0, 1.0, jnp.where(kk == 1, 4.0, jnp.where(kk == 2, 1.0, 0.0))) / 6.0
    c1 = jnp.where(kk == 0, -3.0, jnp.where(kk == 2, 3.0, 0.0)) / 6.0
    c2 = jnp.where(kk == 0, 3.0, jnp.where(kk == 1, -6.0, jnp.where(kk == 2, 3.0, 0.0))) / 6.0
    c3 = jnp.where(kk == 0, -1.0, jnp.where(kk == 1, 3.0, jnp.where(kk == 2, -3.0, 1.0))) / 6.0
    half16 = jnp.where(row16 < 8, 0.0, 1.0)
    mod16 = jnp.bitwise_and(row16, 7).astype(F32).astype(BF16)
    iota16 = row16.astype(F32).astype(BF16)
    zero16 = jnp.zeros((16, LANE), BF16)

    def wide16(row):
        return jnp.broadcast_to(row, (16, LANE))

    def build(lane_at, spot):
        at = pl.ds(lane_at, LANE)
        to = pl.ds(spot, LANE)
        resid = resid_s[:, at]
        att4 = att_ref[:, at] * resid
        v8 = jnp.concatenate([att4, att4], axis=0)
        top = rounded(v8)
        v8 = jnp.where(low8, top, v8 - top)
        v16 = jnp.concatenate([v8, v8], axis=0).astype(BF16)
        interval = (rng_ref[:, at] * 256 + knot_ref[:, at]).astype(F32)
        hi = jnp.floor((interval + 0.5) * (1.0 / ATT_BASE))
        lo = interval - hi * ATT_BASE
        hi16 = (wide16(hi) - half16).astype(BF16)
        for t in range(ATT_HI // 2):
            att_a[t * 16:(t + 1) * 16, to] = jnp.where(hi16 == jnp.array(2 * t, BF16), v16, zero16)
        u = jnp.broadcast_to(pos_ref[:, at], (8, LANE))
        w8 = c0 + u * (c1 + u * (c2 + u * c3))
        top = rounded(w8)
        w8 = jnp.where(low8, top, w8 - top)
        los = [wide16(lo + float(k)).astype(BF16) for k in range(4)]
        ws = [wide16(w8[k:k + 1, :]).astype(BF16) for k in range(8)]
        for t in range(8):
            rows = iota16 + jnp.array(16 * t, BF16)
            top_part = zero16
            low_part = zero16
            for k in range(4):
                same = rows == los[k]
                top_part = jnp.where(same, ws[k], top_part)
                low_part = jnp.where(same, ws[4 + k], low_part)
            att_b[t * 16:(t + 1) * 16, to] = top_part
            att_b[128 + t * 16:128 + (t + 1) * 16, to] = low_part
        unit = unit_s[:, at].astype(F32)
        uhi = jnp.floor((unit + 0.5) * (1.0 / CAL_BASE))
        ulo = unit - uhi * CAL_BASE
        same = wide16(uhi).astype(BF16) == mod16
        g8 = [jnp.broadcast_to(cal_ref[p:p + 1, at], (8, LANE)) for p in range(3)]
        r8 = jnp.broadcast_to(resid, (8, LANE))
        terms = [g8[i] * g8[j] for i in range(3) for j in range(i, 3)] + [g8[i] * r8 for i in range(3)]
        for t in range(9):
            top = rounded(terms[t])
            both = jnp.concatenate([top, terms[t] - top], axis=0).astype(BF16)
            cal_a[t * 16:(t + 1) * 16, to] = jnp.where(same, both, zero16)
        ul16 = wide16(ulo).astype(BF16)
        one16 = jnp.ones((16, LANE), BF16)
        for t in range(16):
            rows = iota16 + jnp.array(16 * t, BF16)
            cal_b[t * 16:(t + 1) * 16, to] = jnp.where(rows == ul16, one16, zero16)

    chunk = att_a.shape[1]

    def turn(turn_at, _):
        start = turn_at * chunk
        for j in range(chunk // LANE):
            build(pl.multiple_of(start + j * LANE, LANE), j * LANE)
        att_acc[...] += lax.dot_general(att_a[...], att_b[...], NT, preferred_element_type=F32)
        cal_acc[...] += lax.dot_general(cal_a[...], cal_b[...], NT, preferred_element_type=F32)
        return 0

    lax.fori_loop(0, GRP * SLOT_BLK // chunk, turn, 0)

    @pl.when(step == pl.num_programs(0) - 1)
    def _():
        att_out[...] = jnp.zeros_like(att_out)
        lane = lax.broadcasted_iota(jnp.int32, (4, LANE), 1)
        for h in range(ATT_HI):
            rows = att_acc[h * 8:(h + 1) * 8, :]
            rows = rows[:, :LANE] + rows[:, LANE:]
            piece = rows[0:4] + rows[4:8]
            where, shift = divmod(h * ATT_BASE, LANE)
            turned = pltpu.roll(piece, shift, 1) if shift else piece
            for part in range(2):
                spot = where + part
                if spot >= 64 or (part == 1 and shift == 0):
                    continue
                keep = lane >= shift if part == 0 else lane < shift
                at = slice((spot % 2) * 4, (spot % 2) * 4 + 4)
                att_out[spot // 2, at, :] += jnp.where(keep, turned, 0.0)
        for t in range(9):
            rows = cal_acc[t * 16:(t + 1) * 16, :]
            cal_out[t] = rows[0:8] + rows[8:16]


def obs_call(chunk=640):
    wide = GRP * SLOT_BLK

    def call(block_count, prefit, partials, attitude, position, calib, source, rng, knot, unit):
        blocks = block_count.shape[0]
        steps = blocks // GRP
        row = pl.BlockSpec((1, wide), lambda s, c: (0, s))
        flat = lambda value: value.reshape(1, -1)
        return pl.pallas_call(
            obs_kernel,
            grid_spec=pltpu.PrefetchScalarGridSpec(
                num_scalar_prefetch=1,
                grid=(steps,),
                in_specs=[
                    row,
                    pl.BlockSpec((5, wide), lambda s, c: (0, s)),
                    pl.BlockSpec((4, wide), lambda s, c: (0, s)),
                    row,
                    pl.BlockSpec((3, wide), lambda s, c: (0, s)),
                    row, row, row, row,
                ],
                out_specs=[
                    pl.BlockSpec((5, GRP * SRC_BLK), lambda s, c: (0, s)),
                    pl.BlockSpec((32, 8, LANE), lambda s, c: (0, 0, 0)),
                    pl.BlockSpec((9, 8, 256), lambda s, c: (0, 0, 0)),
                ],
                scratch_shapes=[
                    pltpu.VMEM((8, wide), F32),
                    pltpu.VMEM((GRP, SRC_BLK, SLOT_BLK), BF16),
                    pltpu.VMEM((40, GRP, LANE), F32),
                    pltpu.VMEM((8, GRP, LANE), F32),
                    pltpu.VMEM((1, wide), F32),
                    pltpu.VMEM((1, wide), jnp.int32),
                    pltpu.VMEM((ATT_HI * 8, chunk), BF16),
                    pltpu.VMEM((256, chunk), BF16),
                    pltpu.VMEM((144, chunk), BF16),
                    pltpu.VMEM((256, chunk), BF16),
                    pltpu.VMEM((ATT_HI * 8, 256), F32),
                    pltpu.VMEM((144, 256), F32),
                ],
            ),
            out_shape=[
                jax.ShapeDtypeStruct((5, blocks * SRC_BLK), F32),
                jax.ShapeDtypeStruct((32, 8, LANE), F32),
                jax.ShapeDtypeStruct((9, 8, 256), F32),
            ],
            compiler_params=pltpu.CompilerParams(vmem_limit_bytes=40 * 1024 * 1024),
        )(block_count, flat(prefit), partials, attitude, flat(position), calib, flat(source), flat(rng), flat(knot), flat(unit))

    return call


def join_kernel(recv_ref, inv_ref, decay_ref, send_ref, mul_ref, add_ref):
    total = recv_ref[0]
    for d in range(1, recv_ref.shape[0]):
        total = total + recv_ref[d]
    acc = jnp.zeros((8, 1024), F32)
    for half in range(2):
        for c in range(4):
            spot = half * 4 + c
            col = jnp.broadcast_to(total[spot:spot + 1, :], (LANE, LANE)).T
            first = c * 256 + half * LANE
            for s in range(LANE // 8):
                line = inv_ref[0, first + s * 8:first + s * 8 + 8, :]
                acc = acc + line * jnp.concatenate([col[s * 8:s * 8 + 8, :]] * 8, axis=1)
    flat = jnp.sum(acc, axis=0, keepdims=True)
    solved = jnp.concatenate([flat[:, c * 256:(c + 1) * 256] for c in range(4)], axis=0)
    decay = decay_ref[...]
    mul = decay
    add = jnp.sqrt(1.0 - decay * decay) * solved
    lane = lax.broadcasted_iota(jnp.int32, (4, 256), 1)
    shift = 1
    while shift < 256:
        inside = lane >= shift
        add = add + jnp.where(inside, mul * pltpu.roll(add, shift, 1), 0.0)
        mul = jnp.where(inside, mul * pltpu.roll(mul, shift, 1), mul)
        shift *= 2
    mul_ref[...] = mul
    add_ref[...] = add
    ends = jnp.where(
        lane[:, :LANE] < 64,
        jnp.broadcast_to(mul[:, 255:256], (4, LANE)),
        jnp.broadcast_to(add[:, 255:256], (4, LANE)),
    )
    out = jnp.concatenate([total[8:10], jnp.zeros((2, LANE), F32), ends], axis=0)
    send_ref[...] = jnp.broadcast_to(out[None], send_ref.shape)


def last_kernel(mine_ref, recv_ref, mul_ref, add_ref, att_ref, cal_ref):
    mine = mine_ref[0]
    lane = lax.broadcasted_iota(jnp.int32, (4, LANE), 1)
    state = jnp.zeros((4, LANE), F32)
    for r in range(31):
        ends = recv_ref[r, 4:8, :]
        turned = pltpu.roll(ends, 64, 1)
        longer = jnp.where(lane < 64, ends, turned) * state + jnp.where(lane < 64, turned, ends)
        state = jnp.where(r < mine, longer, state)
    att_ref[...] = add_ref[...] + mul_ref[...] * jnp.concatenate([state, state], axis=1)
    sums = [
        jnp.concatenate([recv_ref[2 * t, 0:2, :], recv_ref[2 * t + 1, 0:2, :]], axis=0)
        for t in range(9)
    ]
    matrix = [[None] * 3 for _ in range(3)]
    slot = 0
    for i in range(3):
        for j in range(i, 3):
            matrix[i][j] = sums[slot] + (1.0 if i == j else 0.0)
            matrix[j][i] = matrix[i][j]
            slot += 1
    answer = spd_solve(matrix, sums[6:9])
    rest = CAL_BASE - LANE
    for p in range(3):
        for par in range(2):
            first = par * CAL_BASE
            cal_ref[p:p + 1, first:first + LANE] = answer[p][2 * par:2 * par + 1, :]
            cal_ref[p:p + 1, first + LANE:first + CAL_BASE] = answer[p][2 * par + 1:2 * par + 2, :rest]


def on_device(
    prefit_resid, source_partials, attitude_partials, spline_position, calib_partials, obs_source,
    block_count, obs_range, obs_knot, obs_unit, given_inverse, knot_decay,
):
    update, att, cal = obs_call(CHUNK)(
        block_count, prefit_resid, source_partials, attitude_partials, spline_position,
        calib_partials, obs_source, obs_range, obs_knot, obs_unit,
    )
    rows = cal.reshape(9, 4, 2, 2, LANE).transpose(0, 2, 1, 3, 4).reshape(18, 4, 2, LANE)
    rows = jnp.pad(rows, ((0, 14), (0, 0), (0, 0), (0, 0)))
    packed = jnp.concatenate([jnp.broadcast_to(att[:, None], (32, 4, 8, LANE)), rows], axis=2)
    recv = lax.all_to_all(packed.reshape(128, 10, LANE), ("wide", "narrow"), 0, 0)
    big = pltpu.CompilerParams(vmem_limit_bytes=40 * 1024 * 1024)
    small = jax.ShapeDtypeStruct((4, 256), F32)
    send, mul, add = pl.pallas_call(
        join_kernel,
        out_shape=[jax.ShapeDtypeStruct((32, 8, LANE), F32), small, small],
        compiler_params=big,
    )(recv, given_inverse, knot_decay)
    again = lax.all_to_all(send, "wide", 0, 0)
    mine = lax.axis_index("wide").reshape(1).astype(jnp.int32)
    att_update, cal_update = pl.pallas_call(
        last_kernel,
        in_specs=[pl.BlockSpec(memory_space=pltpu.SMEM)] + [pl.BlockSpec(memory_space=pltpu.VMEM)] * 3,
        out_shape=[small, jax.ShapeDtypeStruct((3, 504), F32)],
    )(mine, again, mul, add)
    return update, att_update, cal_update


def solution(mesh):
    both = ("wide", "narrow")
    placed = (
        P(both), P(None, both), P(None, both), P(both), P(None, both), P(both),
        P(both), P(both), P(both), P(both), P("wide", None, None), P(None, "wide"),
    )
    return jax.shard_map(
        on_device,
        mesh=mesh,
        in_specs=placed,
        out_specs=(P(None, both), P(None, "wide"), P(None, "narrow")),
        check_vma=False,
    )
```

time: 651 us -> 104 us (0.16)
  matrix products: 302 us -> 0 us
  local copies, waits for them, and re-layouts: 94.4 us -> 11.6 us
  other arithmetic: 81 us -> 0.09 us
  waiting for transfers between devices: 75 us -> 7.78 us
  Pallas kernels: 0 us -> 48.3 us
  blocking collectives: 74.7 us -> 31.1 us
  between operations: 17 us -> 0.71 us
    dot_general x43 -> x0, matrix products: 302 us -> none  [the longest x40 231 us: accumulate(): jnp.dot(left_rows, second_hot, precision=lax.Precision.HIGHEST)]
    unnamed x3 -> x0, waiting for transfers between devices: 75 us -> none
    unnamed x1 -> x0, blocking collectives: 66.3 us -> none
    dynamic_slice x80 -> x0, local copies, waits for them, and re-layouts: 60.4 us -> none  [the longest x40 27.9 us: accumulate(): lax.dynamic_slice_in_dim(second_ids, starting_offset, piece_size, 0)]
    mul x27 -> x0, other arithmetic: 54.5 us -> none  [the longest x20 49.4 us: accumulate(): value_piece[:, None, :] * first_hot[None, :, :]]
    pallas_call x0 -> x3, Pallas kernels: none -> 48.3 us  [the longest x1 44.9 us: call(): pl.pallas_call(obs_kernel, grid_spec=pltpu.PrefetchScalarGridSpec(num_sca...]
    all_to_all x0 -> x1, blocking collectives: none -> 31.1 us  [on_device(): lax.all_to_all(packed.reshape(128, 10, LANE), ('wide', 'narrow'), 0, 0)]
    another operation x4 -> x0, local copies, waits for them, and re-layouts: 17 us -> none  [the longest x1 12.2 us: on_device(): stacked = jnp.stack(quantities).reshape(20, blocks, SLOT_BLK)]
  transfers between devices with their start and end apart: 2 -> 1, of which waited for: 1 -> 1; matrix products, arithmetic and copies ran while one was open for 32% -> 0% of each run, Pallas kernels for 0% -> 0%
where the time goes in v1:
time: 104 us; the launch traced here: 103 us
  Pallas kernels  48.3 us (46%)
  blocking collectives  31.1 us (30%)
  local copies, waits for them, and re-layouts  11.6 us (11%)
  waiting for transfers between devices  7.78 us (7%)
  starting transfers between devices  3.77 us (4%)
    pallas_call x1, Pallas kernels, call(): pl.pallas_call(obs_kernel, grid_spec=pltpu.PrefetchScalarGridSpec(num_sca...  44.9 us
    all_to_all x1, blocking collectives, on_device(): lax.all_to_all(packed.reshape(128, 10, LANE), ('wide', 'narrow'), 0, 0)  31.1 us
    unnamed x30, local copies, waits for them, and re-layouts  11.5 us
    all_to_all x1, waiting for transfers between devices, on_device(): again = lax.all_to_all(send, 'wide', 0, 0)  7.78 us
    all_to_all x1, starting transfers between devices, on_device(): again = lax.all_to_all(send, 'wide', 0, 0)  3.77 us
  transfers between devices with their start and end apart: 1, of which 1 were waited for; matrix products, arithmetic and copies ran while one was open for 0% of the time, Pallas kernels for 0%

profile of v1, /device:TPU:1, one launch (start us, length us, event | category | flops | bytes accessed | tf_op | source)
XLA Modules:
  0.0 103.3 jit_solution(15104044223103307066)
XLA Ops:
  0.6 0.0 copy-start.12
  0.6 0.0 copy-start.1
  0.7 1.3 %copy-done.1 = f32[5,40960]{1,0:T(8,128)S(1)} copy-done((f32[5,40960]{1,0:T(8,128)S(1)}, f32[5,40960]{1,0:T(8,128)}, u32[]{:S(2)}) %copy-start.1) | copy-done | bytes 819224
  2.0 0.0 copy-start.2
  2.0 1.1 %copy-done.2 = f32[4,40960]{1,0:T(4,128)S(1)} copy-done((f32[4,40960]{1,0:T(4,128)S(1)}, f32[4,40960]{1,0:T(4,128)}, u32[]{:S(2)}) %copy-start.2) | copy-done | bytes 655384
  3.1 0.0 copy-start.3
  3.1 1.1 %copy-done.3 = f32[3,40960]{1,0:T(4,128)S(1)} copy-done((f32[3,40960]{1,0:T(4,128)S(1)}, f32[3,40960]{1,0:T(4,128)}, u32[]{:S(2)}) %copy-start.3) | copy-done | bytes 491544
  4.1 0.0 copy-start.4
  4.1 0.9 copy-done.4
  5.1 0.0 copy-start.5
  5.1 0.9 copy-done.5
  6.0 0.0 copy-start.6
  6.0 0.9 copy-done.6
  6.9 0.0 copy-start.7
  6.9 0.9 copy-done.7
  7.8 0.0 copy-start.8
  7.8 0.9 copy-done.8
  8.7 0.0 copy-start.9
  8.7 0.9 copy-done.9
  9.6 0.0 copy-start.13
  9.6 0.7 copy-done.13
  10.3 44.9 %shard_map.139 = (f32[5,8192]{1,0:T(8,128)}, f32[32,8,128]{2,1,0:T(8,128)S(1)}, f32[9,8,256]{2,1,0:T(8,128)S(1)}) custom-call(s32[64]{0:T(128)S(1)} %copy-done.13, f32[1,40960]{1,0:T(1,128)S(1)} %bitcast.10, f32[5,40960]{1,0:T(8,128)S(1)} %copy-done.1, f32[4,40960]{1,0:T(4,128)S(1)} %copy-done.2, f32[1,40960]{1,0:T(1,128)S(1)} %bitcast.11, ...), custom_call_target="tpu_custom_call" | custom-call | tf_op jit(solution)/shard_map/pallas_call | solution.py:223
  55.2 0.0 copy-start
  55.3 0.1 select_maximum_fusion
  55.4 31.1 %all_to_all.10.recv_ref = f32[128,10,128]{2,1,0:T(8,128)S(1)} all-to-all(f32[128,10,128]{2,1,0:T(8,128)S(1)} %bitcast.16), channel_id=1, replica_groups=mesh['wide'=32,'narrow'=4] {'wide','narrow'}, dimensions={0} | all-to-all | bytes 1310720 | tf_op jit(solution)/shard_map/all_to_all | solution.py:344
  86.5 0.0 copy-done.12
  86.5 0.0 copy-done
  86.5 1.7 %shard_map.140 = (f32[32,8,128]{2,1,0:T(8,128)}, f32[4,256]{1,0:T(4,128)S(1)}, f32[4,256]{1,0:T(4,128)S(1)}) custom-call(f32[128,10,128]{2,1,0:T(8,128)S(1)} %all_to_all.10.recv_ref, f32[1,1024,1024]{2,1,0:T(8,128)S(1)} %copy-done, f32[4,256]{1,0:T(4,128)S(1)} %copy-done.12), custom_call_target="tpu_custom_call" | custom-call | tf_op jit(solution)/shard_map/pallas_call | solution.py:347
  88.2 0.0 copy-start.10
  88.2 0.6 copy-done.10
  88.8 0.0 copy-start.11
  88.8 0.6 copy-done.11
  89.4 3.8 %all-to-all-start.1 = ((f32[32,8,128]{2,1,0:T(8,128)}), f32[32,8,128]{2,1,0:T(8,128)S(1)}, u32[]{:S(2)}, u32[]{:S(2)}) async-start(f32[32,8,128]{2,1,0:T(8,128)} %get-tuple-element.14), calls=%async_computation.1 | async-start | bytes 262144 | tf_op jit(solution)/shard_map/all_to_all | solution.py:352
  93.2 7.8 %all-to-all-done.1.recv_ref = f32[32,8,128]{2,1,0:T(8,128)S(1)} async-done(((f32[32,8,128]{2,1,0:T(8,128)}), f32[32,8,128]{2,1,0:T(8,128)S(1)}, u32[]{:S(2)}, u32[]{:S(2)}) %all-to-all-start.1) | async-done | bytes 131104 | tf_op jit(solution)/shard_map/all_to_all | solution.py:352
  101.0 0.0 copy-start.14
  101.0 0.7 copy-done.14
  101.6 1.7 %shard_map.141 = (f32[4,256]{1,0:T(4,128)}, f32[3,504]{1,0:T(4,128)}) custom-call(s32[1]{0:T(128)} %bitcast.6.mine_ref, f32[32,8,128]{2,1,0:T(8,128)} %copy-done.14, f32[4,256]{1,0:T(4,128)} %copy-done.10, f32[4,256]{1,0:T(4,128)} %copy-done.11), custom_call_target="tpu_custom_call" | custom-call | tf_op jit(solution)/shard_map/pallas_call | solution.py:354
  (3 shorter events, 0.1 us)
Async XLA Ops:
  0.6 85.9 %copy-start.12 = (f32[4,256]{1,0:T(4,128)S(1)}, f32[4,256]{1,0:T(4,128)}, u32[]{:S(2)}) copy-start(f32[4,256]{1,0:T(4,128)} %decay_ref.1) | copy-start | bytes 12292
  0.6 1.3 %copy-start.1 = (f32[5,40960]{1,0:T(8,128)S(1)}, f32[5,40960]{1,0:T(8,128)}, u32[]{:S(2)}) copy-start(f32[5,40960]{1,0:T(8,128)} %par_ref.1) | copy-start | bytes 2457604
  2.0 1.1 %copy-start.2 = (f32[4,40960]{1,0:T(4,128)S(1)}, f32[4,40960]{1,0:T(4,128)}, u32[]{:S(2)}) copy-start(f32[4,40960]{1,0:T(4,128)} %att_ref.1) | copy-start | bytes 1966084
  3.1 1.1 %copy-start.3 = (f32[3,40960]{1,0:T(4,128)S(1)}, f32[3,40960]{1,0:T(4,128)}, u32[]{:S(2)}) copy-start(f32[3,40960]{1,0:T(4,128)} %cal_ref.1) | copy-start | bytes 1474564
  4.1 0.9 copy-start.4
  5.1 0.9 copy-start.5
  6.0 0.9 copy-start.6
  6.9 0.9 copy-start.7
  7.8 0.9 copy-start.8
  8.7 0.9 copy-start.9
  9.6 0.7 copy-start.13
  55.2 31.2 %copy-start = (f32[1,1024,1024]{2,1,0:T(8,128)S(1)}, f32[1,1024,1024]{2,1,0:T(8,128)}, u32[]{:S(2)}) copy-start(f32[1,1024,1024]{2,1,0:T(8,128)} %inv_ref.1) | copy-start | bytes 12582916
  88.2 0.6 copy-start.10
  88.8 0.6 copy-start.11
  89.4 11.6 %all-to-all-start.1 = ((f32[32,8,128]{2,1,0:T(8,128)}), f32[32,8,128]{2,1,0:T(8,128)S(1)}, u32[]{:S(2)}, u32[]{:S(2)}) async-start(f32[32,8,128]{2,1,0:T(8,128)} %get-tuple-element.14), calls=%async_computation.1 | async-start | bytes 262144 | tf_op jit(solution)/shard_map/all_to_all | solution.py:352
  101.0 0.7 copy-start.14

commit v2 on v1

--- a/solution.py
+++ b/solution.py
@@ -10,6 +10,7 @@
 CAL = 2016
 GRP = 8
 CHUNK = 1280
+VMEM_OBS = 60 * 1024 * 1024
 LANE = 128
 ATT_BASE = 125
 ATT_HI = 66
@@ -64,8 +65,8 @@
 
 def obs_kernel(
     count_ref, pre_ref, par_ref, att_ref, pos_ref, cal_ref, src_ref, rng_ref, knot_ref, unit_ref,
-    upd_ref, att_out, cal_out,
-    tile_s, hot_s, sums_s, upd_s, resid_s, unit_s, att_a, att_b, cal_a, cal_b, att_acc, cal_acc,
+    upd_ref, att_out,
+    tile_s, hot_s, sums_s, upd_s, resid_s, unit_s, att_a, att_b, cal_a, cal_b, att_acc, cal_acc, cal_sum,
 ):
     step = pl.program_id(0)
     row8 = lax.broadcasted_iota(jnp.int32, (8, LANE), 0)
@@ -209,7 +210,12 @@
                 att_out[spot // 2, at, :] += jnp.where(keep, turned, 0.0)
         for t in range(9):
             rows = cal_acc[t * 16:(t + 1) * 16, :]
-            cal_out[t] = rows[0:8] + rows[8:16]
+            rows = rows[0:8] + rows[8:16]
+            for half in range(2):
+                cal_sum[half] = rows[:, half * LANE:(half + 1) * LANE]
+                for par in range(2):
+                    spot = 8 + half * 4
+                    att_out[2 * t + par, spot:spot + 4, :] = cal_sum[half, pl.ds(par, 4, stride=2), :]
 
 
 def obs_call(chunk=640):
@@ -235,8 +241,7 @@
                 ],
                 out_specs=[
                     pl.BlockSpec((5, GRP * SRC_BLK), lambda s, c: (0, s)),
-                    pl.BlockSpec((32, 8, LANE), lambda s, c: (0, 0, 0)),
-                    pl.BlockSpec((9, 8, 256), lambda s, c: (0, 0, 0)),
+                    pl.BlockSpec((32, 16, LANE), lambda s, c: (0, 0, 0)),
                 ],
                 scratch_shapes=[
                     pltpu.VMEM((8, wide), F32),
@@ -251,23 +256,23 @@
                     pltpu.VMEM((256, chunk), BF16),
                     pltpu.VMEM((ATT_HI * 8, 256), F32),
                     pltpu.VMEM((144, 256), F32),
+                    pltpu.VMEM((2, 8, LANE), F32),
                 ],
             ),
             out_shape=[
                 jax.ShapeDtypeStruct((5, blocks * SRC_BLK), F32),
-                jax.ShapeDtypeStruct((32, 8, LANE), F32),
-                jax.ShapeDtypeStruct((9, 8, 256), F32),
+                jax.ShapeDtypeStruct((32, 16, LANE), F32),
             ],
-            compiler_params=pltpu.CompilerParams(vmem_limit_bytes=40 * 1024 * 1024),
+            compiler_params=pltpu.CompilerParams(vmem_limit_bytes=VMEM_OBS),
         )(block_count, flat(prefit), partials, attitude, flat(position), calib, flat(source), flat(rng), flat(knot), flat(unit))
 
     return call
 
 
-def join_kernel(recv_ref, inv_ref, decay_ref, send_ref, mul_ref, add_ref):
-    total = recv_ref[0]
-    for d in range(1, recv_ref.shape[0]):
-        total = total + recv_ref[d]
+def join_kernel(group_ref, own_ref, one_ref, two_ref, three_ref, inv_ref, decay_ref, send_ref, mul_ref, add_ref, rows_s):
+    total = own_ref[...] + one_ref[...] + two_ref[...] + three_ref[...]
+    rows_s[...] = total
+    group = group_ref[0]
     acc = jnp.zeros((8, 1024), F32)
     for half in range(2):
         for c in range(4):
@@ -296,7 +301,7 @@
         jnp.broadcast_to(mul[:, 255:256], (4, LANE)),
         jnp.broadcast_to(add[:, 255:256], (4, LANE)),
     )
-    out = jnp.concatenate([total[8:10], jnp.zeros((2, LANE), F32), ends], axis=0)
+    out = jnp.concatenate([rows_s[pl.ds(8 + group, 1), :], rows_s[pl.ds(12 + group, 1), :], jnp.zeros((2, LANE), F32), ends], axis=0)
     send_ref[...] = jnp.broadcast_to(out[None], send_ref.shape)
 
 
@@ -334,27 +339,32 @@
     prefit_resid, source_partials, attitude_partials, spline_position, calib_partials, obs_source,
     block_count, obs_range, obs_knot, obs_unit, given_inverse, knot_decay,
 ):
-    update, att, cal = obs_call(CHUNK)(
+    update, packed = obs_call(CHUNK)(
         block_count, prefit_resid, source_partials, attitude_partials, spline_position,
         calib_partials, obs_source, obs_range, obs_knot, obs_unit,
     )
-    rows = cal.reshape(9, 4, 2, 2, LANE).transpose(0, 2, 1, 3, 4).reshape(18, 4, 2, LANE)
-    rows = jnp.pad(rows, ((0, 14), (0, 0), (0, 0), (0, 0)))
-    packed = jnp.concatenate([jnp.broadcast_to(att[:, None], (32, 4, 8, LANE)), rows], axis=2)
-    recv = lax.all_to_all(packed.reshape(128, 10, LANE), ("wide", "narrow"), 0, 0)
-    big = pltpu.CompilerParams(vmem_limit_bytes=40 * 1024 * 1024)
+    own = jnp.sum(lax.all_to_all(packed, "wide", 0, 0), axis=0)
+    others = [
+        lax.ppermute(own, "narrow", [(i, (i + shift) % 4) for i in range(4)]) for shift in (1, 2, 3)
+    ]
+    group = lax.axis_index("narrow").reshape(1).astype(jnp.int32)
+    scalar = pl.BlockSpec(memory_space=pltpu.SMEM)
+    vector = pl.BlockSpec(memory_space=pltpu.VMEM)
     small = jax.ShapeDtypeStruct((4, 256), F32)
     send, mul, add = pl.pallas_call(
         join_kernel,
+        in_specs=[scalar] + [vector] * 6,
         out_shape=[jax.ShapeDtypeStruct((32, 8, LANE), F32), small, small],
-        compiler_params=big,
-    )(recv, given_inverse, knot_decay)
+        scratch_shapes=[pltpu.VMEM((16, LANE), F32)],
+        compiler_params=pltpu.CompilerParams(vmem_limit_bytes=16 * 1024 * 1024),
+    )(group, own, *others, given_inverse, knot_decay)
     again = lax.all_to_all(send, "wide", 0, 0)
     mine = lax.axis_index("wide").reshape(1).astype(jnp.int32)
     att_update, cal_update = pl.pallas_call(
         last_kernel,
-        in_specs=[pl.BlockSpec(memory_space=pltpu.SMEM)] + [pl.BlockSpec(memory_space=pltpu.VMEM)] * 3,
+        in_specs=[scalar] + [vector] * 3,
         out_shape=[small, jax.ShapeDtypeStruct((3, 504), F32)],
+        compiler_params=pltpu.CompilerParams(vmem_limit_bytes=16 * 1024 * 1024),
     )(mine, again, mul, add)
     return update, att_update, cal_update
 

time: 104 us -> 90 us (0.87)
  blocking collectives: 31.1 us -> 18.6 us
  local copies, waits for them, and re-layouts: 11.6 us -> 2.19 us
  starting transfers between devices: 3.77 us -> 10 us
  waiting for transfers between devices: 7.78 us -> 9.44 us
    all_to_all x1, blocking collectives: 31.1 us -> 18.6 us  [on_device(): own = jnp.sum(lax.all_to_all(packed, 'wide', 0, 0), axis=0)]
    unnamed x30 -> x4, local copies, waits for them, and re-layouts: 11.5 us -> 2.19 us
    ppermute x0 -> x3, starting transfers between devices: none -> 4.88 us  [on_device(): lax.ppermute(own, 'narrow', [(i, (i + shift) % 4) for i in range(4)])]
    ppermute x0 -> x3, waiting for transfers between devices: none -> 1.62 us  [on_device(): lax.ppermute(own, 'narrow', [(i, (i + shift) % 4) for i in range(4)])]
    pallas_call x1, Pallas kernels: 44.9 us -> 46.4 us  [call(): pl.pallas_call(obs_kernel, grid_spec=pltpu.PrefetchScalarGridSpec(num_sca...]
    all_to_all x1, starting transfers between devices: 3.77 us -> 5.11 us  [on_device(): again = lax.all_to_all(send, 'wide', 0, 0)]
  transfers between devices with their start and end apart: 1 -> 4, of which waited for: 1 -> 3; matrix products, arithmetic and copies ran while one was open for 0% -> 0% of each run, Pallas kernels for 0% -> 0%
where the time goes in v2:
time: 90 us; the launch traced here: 89.7 us
  Pallas kernels  48.7 us (54%)
  blocking collectives  18.6 us (21%)
  starting transfers between devices  10 us (11%)
  waiting for transfers between devices  9.44 us (10%)
  local copies, waits for them, and re-layouts  2.19 us (2%)
    pallas_call x1, Pallas kernels, call(): pl.pallas_call(obs_kernel, grid_spec=pltpu.PrefetchScalarGridSpec(num_sca...  46.4 us
    all_to_all x1, blocking collectives, on_device(): own = jnp.sum(lax.all_to_all(packed, 'wide', 0, 0), axis=0)  18.6 us
    all_to_all x1, waiting for transfers between devices, on_device(): again = lax.all_to_all(send, 'wide', 0, 0)  7.81 us
    all_to_all x1, starting transfers between devices, on_device(): again = lax.all_to_all(send, 'wide', 0, 0)  5.11 us
    ppermute x3, starting transfers between devices, on_device(): lax.ppermute(own, 'narrow', [(i, (i + shift) % 4) for i in range(4)])  4.88 us
    unnamed x4, local copies, waits for them, and re-layouts  2.19 us
  transfers between devices with their start and end apart: 4, of which 3 were waited for; matrix products, arithmetic and copies ran while one was open for 0% of the time, Pallas kernels for 0%

profile of v2, /device:TPU:1, one launch (start us, length us, event | category | flops | bytes accessed | tf_op | source)
XLA Modules:
  0.0 89.7 jit_solution(13713078782723251089)
XLA Ops:
  0.6 0.0 copy-start.1
  0.6 46.4 %shard_map.139 = (f32[5,8192]{1,0:T(8,128)}, f32[32,16,128]{2,1,0:T(8,128)}) custom-call(s32[64]{0:T(128)} %count_ref.1, f32[1,40960]{1,0:T(1,128)} %bitcast.8, f32[5,40960]{1,0:T(8,128)} %par_ref.1, f32[4,40960]{1,0:T(4,128)} %att_ref.1, f32[1,40960]{1,0:T(1,128)} %bitcast.9, f32[3,40960]{1,0:T(4,128)} %cal_ref.1, s32[1,40960]{1,0:T(1,128)} %bitcast.10, ...), custom_call_target="tpu_custom_call" | custom-call | tf_op jit(solution)/shard_map/pallas_call | solution.py:229
  47.0 18.6 %all_to_all.10 = f32[32,16,128]{2,1,0:T(8,128)S(1)} all-to-all(f32[32,16,128]{2,1,0:T(8,128)} %get-tuple-element.11), channel_id=1, replica_groups=mesh['wide'=32,'narrow'=4] {'wide'}, dimensions={0} | all-to-all | bytes 524288 | tf_op jit(solution)/shard_map/all_to_all | solution.py:346
  65.6 1.3 %collective-permute-start = (f32[16,128]{1,0:T(8,128)S(1)}, f32[16,128]{1,0:T(8,128)S(1)}, u32[]{:S(2)}, u32[]{:S(2)}) collective-permute-start(f32[16,128]{1,0:T(8,128)S(1)} %reduce_sum.9.own_ref), channel_id=1, source_target_pairs={{0,1},{1,2},{2,3},{3,0},{4,5},{5,6},{6,7},{7,4},{8,9},{9,10},{10,1... | collective-permute-start | bytes 24584 | tf_op jit(solution)/shard_map/ppermute | solution.py:348
  66.9 2.4 %collective-permute-start.1 = (f32[16,128]{1,0:T(8,128)S(1)}, f32[16,128]{1,0:T(8,128)S(1)}, u32[]{:S(2)}, u32[]{:S(2)}) collective-permute-start(f32[16,128]{1,0:T(8,128)S(1)} %reduce_sum.9.own_ref), channel_id=1, source_target_pairs={{0,2},{1,3},{2,0},{3,1},{4,6},{5,7},{6,4},{7,5},{8,10},{9,11},{10,... | collective-permute-start | bytes 24584 | tf_op jit(solution)/shard_map/ppermute | solution.py:348
  69.4 1.2 %collective-permute-start.2 = (f32[16,128]{1,0:T(8,128)S(1)}, f32[16,128]{1,0:T(8,128)S(1)}, u32[]{:S(2)}, u32[]{:S(2)}) collective-permute-start(f32[16,128]{1,0:T(8,128)S(1)} %reduce_sum.9.own_ref), channel_id=1, source_target_pairs={{0,3},{1,0},{2,1},{3,2},{4,7},{5,4},{6,5},{7,6},{8,11},{9,8},{10,9... | collective-permute-start | bytes 24584 | tf_op jit(solution)/shard_map/ppermute | solution.py:348
  70.5 0.0 collective-permute-done.one_ref
  70.5 0.4 collective-permute-done.1.two_ref
  70.9 1.2 %collective-permute-done.2.three_ref = f32[16,128]{1,0:T(8,128)S(1)} collective-permute-done((f32[16,128]{1,0:T(8,128)S(1)}, f32[16,128]{1,0:T(8,128)S(1)}, u32[]{:S(2)}, u32[]{:S(2)}) %collective-permute-start.2) | collective-permute-done | bytes 8224 | tf_op jit(solution)/shard_map/ppermute | solution.py:348
  72.2 0.0 copy-done.1
  72.2 0.0 copy-start
  72.2 2.2 %copy-done = f32[1,1024,1024]{2,1,0:T(8,128)S(1)} copy-done((f32[1,1024,1024]{2,1,0:T(8,128)S(1)}, f32[1,1024,1024]{2,1,0:T(8,128)}, u32[]{:S(2)}) %copy-start) | copy-done | bytes 4194328
  74.3 1.6 %shard_map.140 = (f32[32,8,128]{2,1,0:T(8,128)}, f32[4,256]{1,0:T(4,128)S(1)}, f32[4,256]{1,0:T(4,128)S(1)}) custom-call(s32[1]{0:T(128)} %bitcast.7.group_ref, f32[16,128]{1,0:T(8,128)S(1)} %reduce_sum.9.own_ref, f32[16,128]{1,0:T(8,128)S(1)} %collective-permute-done.one_ref, f32[16,128]{1,0:T(8,128)S(1)} %collective-permute-done.1.two_ref, ...), custom_call_target="tpu_custom_call" | custom-call | tf_op jit(solution)/shard_map/pallas_call | solution.py:354
  76.0 5.1 %all-to-all-start.1 = ((f32[32,8,128]{2,1,0:T(8,128)}), f32[32,8,128]{2,1,0:T(8,128)S(1)}, u32[]{:S(2)}, u32[]{:S(2)}) async-start(f32[32,8,128]{2,1,0:T(8,128)} %get-tuple-element.12), calls=%async_computation.1 | async-start | bytes 262144 | tf_op jit(solution)/shard_map/all_to_all | solution.py:361
  81.1 7.8 %all-to-all-done.1.recv_ref = f32[32,8,128]{2,1,0:T(8,128)S(1)} async-done(((f32[32,8,128]{2,1,0:T(8,128)}), f32[32,8,128]{2,1,0:T(8,128)S(1)}, u32[]{:S(2)}, u32[]{:S(2)}) %all-to-all-start.1) | async-done | bytes 131104 | tf_op jit(solution)/shard_map/all_to_all | solution.py:361
  88.9 0.7 shard_map.141
  (1 shorter events, 0.0 us)
Async XLA Ops:
  0.6 71.5 %copy-start.1 = (f32[4,256]{1,0:T(4,128)S(1)}, f32[4,256]{1,0:T(4,128)}, u32[]{:S(2)}) copy-start(f32[4,256]{1,0:T(4,128)} %decay_ref.1) | copy-start | bytes 12292
  65.6 4.9 %collective-permute-start = (f32[16,128]{1,0:T(8,128)S(1)}, f32[16,128]{1,0:T(8,128)S(1)}, u32[]{:S(2)}, u32[]{:S(2)}) collective-permute-start(f32[16,128]{1,0:T(8,128)S(1)} %reduce_sum.9.own_ref), channel_id=1, source_target_pairs={{0,1},{1,2},{2,3},{3,0},{4,5},{5,6},{6,7},{7,4},{8,9},{9,10},{10,1... | collective-permute-start | bytes 24584 | tf_op jit(solution)/shard_map/ppermute | solution.py:348
  66.9 4.0 %collective-permute-start.1 = (f32[16,128]{1,0:T(8,128)S(1)}, f32[16,128]{1,0:T(8,128)S(1)}, u32[]{:S(2)}, u32[]{:S(2)}) collective-permute-start(f32[16,128]{1,0:T(8,128)S(1)} %reduce_sum.9.own_ref), channel_id=1, source_target_pairs={{0,2},{1,3},{2,0},{3,1},{4,6},{5,7},{6,4},{7,5},{8,10},{9,11},{10,... | collective-permute-start | bytes 24584 | tf_op jit(solution)/shard_map/ppermute | solution.py:348
  69.4 2.8 %collective-permute-start.2 = (f32[16,128]{1,0:T(8,128)S(1)}, f32[16,128]{1,0:T(8,128)S(1)}, u32[]{:S(2)}, u32[]{:S(2)}) collective-permute-start(f32[16,128]{1,0:T(8,128)S(1)} %reduce_sum.9.own_ref), channel_id=1, source_target_pairs={{0,3},{1,0},{2,1},{3,2},{4,7},{5,4},{6,5},{7,6},{8,11},{9,8},{10,9... | collective-permute-start | bytes 24584 | tf_op jit(solution)/shard_map/ppermute | solution.py:348
  72.2 2.2 %copy-start = (f32[1,1024,1024]{2,1,0:T(8,128)S(1)}, f32[1,1024,1024]{2,1,0:T(8,128)}, u32[]{:S(2)}) copy-start(f32[1,1024,1024]{2,1,0:T(8,128)} %inv_ref.1) | copy-start | bytes 12582916
  76.0 12.9 %all-to-all-start.1 = ((f32[32,8,128]{2,1,0:T(8,128)}), f32[32,8,128]{2,1,0:T(8,128)S(1)}, u32[]{:S(2)}, u32[]{:S(2)}) async-start(f32[32,8,128]{2,1,0:T(8,128)} %get-tuple-element.12), calls=%async_computation.1 | async-start | bytes 262144 | tf_op jit(solution)/shard_map/all_to_all | solution.py:361

commit v3 on v2

v3 whole, which is shorter than its diff:
```python
import jax
import jax.numpy as jnp
from jax import lax
from jax.experimental import pallas as pl
from jax.experimental.pallas import tpu as pltpu
from jax.sharding import PartitionSpec as P

SRC_BLK = 128
SLOT_BLK = 640
CAL = 2016
GRP = 8
TURN = 16
VMEM_OBS = 60 * 1024 * 1024
LANE = 128
ATT_BASE = 125
ATT_HI = 68
CAL_BASE = 252
CAL_HI = 8
F32 = jnp.float32
BF16 = jnp.bfloat16


def rounded(value):
    return value.astype(BF16).astype(F32)


def split3(value):
    top = rounded(value)
    rest = value - top
    mid = rounded(rest)
    return top, mid, rest - mid


def spd_solve(matrix, target):
    order = len(target)
    lower = [[None] * order for _ in range(order)]
    inv = [None] * order
    for col in range(order):
        pivot = matrix[col][col]
        for k in range(col):
            pivot = pivot - lower[col][k] * lower[col][k]
        inv[col] = 1.0 / jnp.sqrt(pivot)
        for row in range(col + 1, order):
            entry = matrix[row][col]
            for k in range(col):
                entry = entry - lower[row][k] * lower[col][k]
            lower[row][col] = entry * inv[col]
    forward = []
    for row in range(order):
        running = target[row]
        for k in range(row):
            running = running - lower[row][k] * forward[k]
        forward.append(running * inv[row])
    answer = [None] * order
    for row in reversed(range(order)):
        running = forward[row]
        for k in range(row + 1, order):
            running = running - lower[k][row] * answer[k]
        answer[row] = running * inv[row]
    return answer


NT = (((1,), (1,)), ((), ()))


def obs_kernel(
    count_ref, pre_hbm, par_hbm, att_hbm, pos_hbm, cal_hbm, src_hbm, rng_hbm, knot_hbm, unit_hbm,
    upd_ref, att_out,
    pre_ref, par_ref, att_ref, pos_ref, cal_ref, src_ref, rng_ref, knot_ref, unit_ref,
    tile_s, sums_s, upd_s, back_s,
    att_acc, cal_acc, cal_sum, start_s, live_s, block_s, sems,
):
    pairs = [
        (pre_hbm, pre_ref), (par_hbm, par_ref), (src_hbm, src_ref), (att_hbm, att_ref), (pos_hbm, pos_ref),
        (cal_hbm, cal_ref), (rng_hbm, rng_ref), (knot_hbm, knot_ref), (unit_hbm, unit_ref),
    ]
    copies = [pltpu.make_async_copy(src, dst, sems.at[i]) for i, (src, dst) in enumerate(pairs)]
    for copy in copies:
        copy.start()
    blocks = count_ref.shape[0]
    tiles = SLOT_BLK // LANE
    row8 = lax.broadcasted_iota(jnp.int32, (8, LANE), 0)
    row16 = lax.broadcasted_iota(jnp.int32, (16, LANE), 0)
    lane1 = lax.broadcasted_iota(jnp.int32, (1, LANE), 1)
    att_out[...] = jnp.zeros_like(att_out)

    def listing(block, spot):
        count = count_ref[block]
        for t in range(tiles):
            start_s[spot + t] = block * SLOT_BLK + t * LANE
            live_s[spot + t] = count - t * LANE
            block_s[spot + t] = block
        return spot + lax.shift_right_logical(count + (LANE - 1), 7)

    used = lax.fori_loop(0, blocks, listing, 0)
    for t in range(TURN):
        start_s[used + t] = 0
        live_s[used + t] = 0
        block_s[used + t] = 0
    turns = lax.div(used + (TURN - 1), TURN)

    for copy in copies[:3]:
        copy.wait()
    low8 = row8 < 4
    kk = jnp.bitwise_and(row8, 3)
    c0 = jnp.where(kk == 0, 1.0, jnp.where(kk == 1, 4.0, jnp.where(kk == 2, 1.0, 0.0))) / 6.0
    c1 = jnp.where(kk == 0, -3.0, jnp.where(kk == 2, 3.0, 0.0)) / 6.0
    c2 = jnp.where(kk == 0, 3.0, jnp.where(kk == 1, -6.0, jnp.where(kk == 2, 3.0, 0.0))) / 6.0
    c3 = jnp.where(kk == 0, -1.0, jnp.where(kk == 1, 3.0, jnp.where(kk == 2, -3.0, 1.0))) / 6.0
    quad16 = lax.shift_right_logical(row16, 2).astype(F32)
    mod16 = jnp.bitwise_and(row16, 7).astype(F32).astype(BF16)
    iota16 = row16.astype(F32).astype(BF16)
    zero16 = jnp.zeros((16, LANE), BF16)
    one16 = jnp.ones((16, LANE), BF16)

    def wide16(row):
        return jnp.broadcast_to(row, (16, LANE))

    def beside(left, right):
        return jnp.concatenate([left, right], axis=1)

    def one_hot(row16, count):
        return [jnp.where(iota16 + jnp.array(16 * t, BF16) == row16, one16, zero16) for t in range(count)]

    def source_tile(block, t):
        at = pl.ds(pl.multiple_of(block * SLOT_BLK + t * LANE, LANE), LANE)
        live = lane1 < count_ref[block] - t * LANE
        ids = jnp.where(live, src_ref[:, at], -1).astype(F32)
        par = par_ref[:, at]
        tile_s[0:5, at] = par
        tile_s[5:6, at] = pre_ref[:, at]
        tile_s[6:8, at] = par[0:2]
        tile = tile_s[:, at]
        turned = [tile] + [pltpu.roll(tile, 8 - d, 0) for d in (1, 2, 3)]
        pieces = []
        for d in (0, 2):
            both = jnp.concatenate([tile * turned[d], tile * turned[d + 1]], axis=0)
            pieces.append([part.astype(BF16) for part in split3(both)])
        return one_hot(wide16(ids).astype(BF16), 8), pieces

    def source_sums(accs):
        def group_sums(group, _):
            for pair in range(GRP // 2):
                unit = pair % 2
                block = group * GRP + 2 * pair
                for t in range(tiles):
                    left_hot, left = source_tile(block, t)
                    right_hot, right = source_tile(block + 1, t)
                    rows = [beside(piece, zero16) for piece in left_hot]
                    rows += [beside(zero16, piece) for piece in right_hot]
                    stage = t % 2 if unit == pair else (t + 1) % 2
                    pltpu.matmul_push_rhs(jnp.concatenate(rows, axis=0), stage, unit, transpose=True)
                    for d in range(2):
                        for k in range(3):
                            pltpu.matmul_acc_lhs(
                                accs[pair][d], beside(left[d][k], right[d][k]), stage if d + k == 0 else None
                            )
            for pair in range(GRP // 2):
                for d in range(2):
                    sums = pltpu.matmul_pop(accs[pair][d])
                    for side in range(2):
                        sums_s[group, 16 * d:16 * d + 16, 2 * pair + side, :] = sums[:, side * LANE:(side + 1) * LANE]
            return 0

        lax.fori_loop(0, blocks // GRP, group_sums, 0)

    pl.run_scoped(
        source_sums, [[pltpu.ACC(pair % 2)((16, 256), F32) for _ in range(2)] for pair in range(GRP // 2)]
    )

    matrix = [[None] * 5 for _ in range(5)]
    for i in range(5):
        for j in range(i, 5):
            apart = j - i
            spot = apart * 8 + i if apart < 4 else 20
            entry = sums_s[:, spot] + (1.0 if i == j else 0.0)
            matrix[i][j] = entry
            matrix[j][i] = entry
    answer = spd_solve(matrix, [sums_s[:, spot] for spot in (13, 21, 26, 19, 12)])
    for p in range(5):
        upd_s[p] = answer[p]
    upd_s[5] = jnp.full(upd_s.shape[1:], -1.0, F32)
    upd_s[6] = jnp.zeros(upd_s.shape[1:], F32)
    upd_s[7] = jnp.zeros(upd_s.shape[1:], F32)
    for block in range(blocks):
        mine = upd_s[:, block // GRP, block % GRP, :]
        back_s[block] = mine
        upd_ref[:, block * SRC_BLK:(block + 1) * SRC_BLK] = mine[0:5]
    for copy in copies[3:]:
        copy.wait()

    def tile_rows(entry):
        at = pl.ds(pl.multiple_of(start_s[entry], LANE), LANE)
        live = lane1 < live_s[entry]
        index = jnp.broadcast_to(src_ref[:, at], (8, LANE))
        picked = jnp.take_along_axis(back_s[block_s[entry]], index, axis=1, mode="promise_in_bounds")
        resid = jnp.where(live, -jnp.sum(picked * tile_s[:, at], axis=0, keepdims=True), 0.0)
        att4 = att_ref[:, at] * resid
        v8 = jnp.concatenate([att4, att4], axis=0)
        top8 = rounded(v8)
        rest8 = v8 - top8
        v16 = [jnp.concatenate([part, part], axis=0).astype(BF16) for part in (top8, rest8)]
        interval = (rng_ref[:, at] * 256 + knot_ref[:, at]).astype(F32)
        hi = jnp.floor((interval + 0.5) * (1.0 / ATT_BASE))
        lo = interval - hi * ATT_BASE
        hi16 = (wide16(hi) - quad16).astype(BF16)
        u = jnp.broadcast_to(pos_ref[:, at], (8, LANE))
        w8 = c0 + u * (c1 + u * (c2 + u * c3))
        top = rounded(w8)
        w8 = jnp.where(low8, top, w8 - top)
        los = [wide16(lo + float(k)).astype(BF16) for k in range(4)]
        ws = [wide16(w8[k:k + 1, :]).astype(BF16) for k in range(8)]
        unit = jnp.where(live, unit_ref[:, at], -1).astype(F32)
        uhi = jnp.floor((unit + 0.5) * (1.0 / CAL_BASE))
        ulo = unit - uhi * CAL_BASE
        same = wide16(uhi).astype(BF16) == mod16
        g8 = [jnp.broadcast_to(cal_ref[p:p + 1, at], (8, LANE)) for p in range(3)]
        r8 = jnp.broadcast_to(resid, (8, LANE))
        terms = [g8[i] * g8[j] for i in range(3) for j in range(i, 3)] + [g8[i] * r8 for i in range(3)]
        pieces = []
        for t in range(9):
            top = rounded(terms[t])
            both = jnp.concatenate([top, terms[t] - top], axis=0).astype(BF16)
            pieces.append(jnp.where(same, both, zero16))
        ul16 = wide16(ulo).astype(BF16)
        return v16, hi16, los, ws, pieces, ul16

    def knot_columns(los, ws):
        tops, lows = [], []
        for t in range(8):
            rows = iota16 + jnp.array(16 * t, BF16)
            top_part = zero16
            low_part = zero16
            for k in range(4):
                same = rows == los[k]
                top_part = jnp.where(same, ws[k], top_part)
                low_part = jnp.where(same, ws[4 + k], low_part)
            tops.append(top_part)
            lows.append(low_part)
        return jnp.concatenate(tops + lows, axis=0)

    def matmuls(att_accs, cal_accs):
        def spend(entry, unit):
            left, right = tile_rows(entry), tile_rows(entry + 1)
            pltpu.matmul_push_rhs(
                beside(knot_columns(left[2], left[3]), knot_columns(right[2], right[3])), 0, unit, transpose=True
            )
            for t in range(ATT_HI // 4):
                step = jnp.array(4 * t, BF16)
                same = [side[1] == step for side in (left, right)]
                for k in range(2):
                    rows = beside(jnp.where(same[0], left[0][k], zero16), jnp.where(same[1], right[0][k], zero16))
                    pltpu.matmul_acc_lhs(att_accs[unit][2 * t + k], rows, 0 if t + k == 0 else None)
            pltpu.matmul_push_rhs(
                beside(jnp.concatenate(one_hot(left[5], 16), axis=0), jnp.concatenate(one_hot(right[5], 16), axis=0)), 1, unit, transpose=True
            )
            for t in range(9):
                pltpu.matmul_acc_lhs(cal_accs[unit][t], beside(left[4][t], right[4][t]), 1 if t == 0 else None)

        def turn(turn_at, _):
            for part in range(TURN // 2):
                spend(turn_at * TURN + 2 * part, part % 2)
            return 0

        lax.fori_loop(0, turns, turn, 0)
        for t in range(ATT_HI // 4):
            parts = [pltpu.matmul_pop(att_accs[unit][2 * t + k]) for unit in range(2) for k in range(2)]
            att_acc[t * 16:(t + 1) * 16, :] = (parts[0] + parts[1]) + (parts[2] + parts[3])
        for t in range(9):
            cal_acc[t * 16:(t + 1) * 16, :] = pltpu.matmul_pop(cal_accs[0][t]) + pltpu.matmul_pop(cal_accs[1][t])

    pl.run_scoped(
        matmuls,
        [[pltpu.ACC(unit)((16, 256), F32) for _ in range(ATT_HI // 2)] for unit in range(2)],
        [[pltpu.ACC(unit)((16, 256), F32) for _ in range(9)] for unit in range(2)],
    )

    lane = lax.broadcasted_iota(jnp.int32, (4, LANE), 1)
    for h in range(ATT_HI):
        rows = att_acc[h * 4:(h + 1) * 4, :]
        piece = rows[:, :LANE] + rows[:, LANE:]
        where, shift = divmod(h * ATT_BASE, LANE)
        turned = pltpu.roll(piece, shift, 1) if shift else piece
        for part in range(2):
            spot = where + part
            if spot >= 64 or (part == 1 and shift == 0):
                continue
            keep = lane >= shift if part == 0 else lane < shift
            at = slice((spot % 2) * 4, (spot % 2) * 4 + 4)
            att_out[spot // 2, at, :] += jnp.where(keep, turned, 0.0)
    for t in range(9):
        rows = cal_acc[t * 16:(t + 1) * 16, :]
        rows = rows[0:8] + rows[8:16]
        for half in range(2):
            cal_sum[half] = rows[:, half * LANE:(half + 1) * LANE]
            for par in range(2):
                spot = 8 + half * 4
                att_out[2 * t + par, spot:spot + 4, :] = cal_sum[half, pl.ds(par, 4, stride=2), :]


def obs_call(block_count, prefit, partials, attitude, position, calib, source, rng, knot, unit):
    blocks = block_count.shape[0]
    count = prefit.shape[0]
    flat = lambda value: value.reshape(1, -1)
    row = lambda kind: pltpu.VMEM((1, count), kind)
    listed = pltpu.SMEM((count // LANE + TURN + 8,), jnp.int32)
    return pl.pallas_call(
        obs_kernel,
        in_specs=[pl.BlockSpec(memory_space=pltpu.SMEM)] + [pl.BlockSpec(memory_space=pl.ANY)] * 9,
        out_specs=[pl.BlockSpec(memory_space=pltpu.VMEM)] * 2,
        out_shape=[
            jax.ShapeDtypeStruct((5, blocks * SRC_BLK), F32),
            jax.ShapeDtypeStruct((32, 16, LANE), F32),
        ],
        scratch_shapes=[
            row(F32), pltpu.VMEM((5, count), F32), pltpu.VMEM((4, count), F32), row(F32),
            pltpu.VMEM((3, count), F32), row(jnp.int32), row(jnp.int32), row(jnp.int32), row(jnp.int32),
            pltpu.VMEM((8, count), F32),
            pltpu.VMEM((blocks // GRP, 32, GRP, LANE), F32),
            pltpu.VMEM((8, blocks // GRP, GRP, LANE), F32),
            pltpu.VMEM((blocks, 8, LANE), F32),
            pltpu.VMEM((ATT_HI * 4, 256), F32),
            pltpu.VMEM((144, 256), F32),
            pltpu.VMEM((2, 8, LANE), F32),
            listed, listed, listed,
            pltpu.SemaphoreType.DMA((9,)),
        ],
        compiler_params=pltpu.CompilerParams(vmem_limit_bytes=VMEM_OBS),
    )(block_count, flat(prefit), partials, attitude, flat(position), calib, flat(source), flat(rng), flat(knot), flat(unit))


def join_kernel(group_ref, own_ref, one_ref, two_ref, three_ref, inv_ref, decay_ref, send_ref, mul_ref, add_ref, rows_s):
    total = own_ref[...] + one_ref[...] + two_ref[...] + three_ref[...]
    rows_s[...] = total
    group = group_ref[0]
    acc = jnp.zeros((8, 1024), F32)
    for half in range(2):
        for c in range(4):
            spot = half * 4 + c
            col = jnp.broadcast_to(total[spot:spot + 1, :], (LANE, LANE)).T
            first = c * 256 + half * LANE
            for s in range(LANE // 8):
                line = inv_ref[0, first + s * 8:first + s * 8 + 8, :]
                acc = acc + line * jnp.concatenate([col[s * 8:s * 8 + 8, :]] * 8, axis=1)
    flat = jnp.sum(acc, axis=0, keepdims=True)
    solved = jnp.concatenate([flat[:, c * 256:(c + 1) * 256] for c in range(4)], axis=0)
    decay = decay_ref[...]
    mul = decay
    add = jnp.sqrt(1.0 - decay * decay) * solved
    lane = lax.broadcasted_iota(jnp.int32, (4, 256), 1)
    shift = 1
    while shift < 256:
        inside = lane >= shift
        add = add + jnp.where(inside, mul * pltpu.roll(add, shift, 1), 0.0)
        mul = jnp.where(inside, mul * pltpu.roll(mul, shift, 1), mul)
        shift *= 2
    mul_ref[...] = mul
    add_ref[...] = add
    ends = jnp.where(
        lane[:, :LANE] < 64,
        jnp.broadcast_to(mul[:, 255:256], (4, LANE)),
        jnp.broadcast_to(add[:, 255:256], (4, LANE)),
    )
    out = jnp.concatenate([rows_s[pl.ds(8 + group, 1), :], rows_s[pl.ds(12 + group, 1), :], jnp.zeros((2, LANE), F32), ends], axis=0)
    send_ref[...] = jnp.broadcast_to(out[None], send_ref.shape)


def last_kernel(mine_ref, recv_ref, mul_ref, add_ref, att_ref, cal_ref):
    mine = mine_ref[0]
    lane = lax.broadcasted_iota(jnp.int32, (4, LANE), 1)
    state = jnp.zeros((4, LANE), F32)
    for r in range(31):
        ends = recv_ref[r, 4:8, :]
        turned = pltpu.roll(ends, 64, 1)
        longer = jnp.where(lane < 64, ends, turned) * state + jnp.where(lane < 64, turned, ends)
        state = jnp.where(r < mine, longer, state)
    att_ref[...] = add_ref[...] + mul_ref[...] * jnp.concatenate([state, state], axis=1)
    sums = [
        jnp.concatenate([recv_ref[2 * t, 0:2, :], recv_ref[2 * t + 1, 0:2, :]], axis=0)
        for t in range(9)
    ]
    matrix = [[None] * 3 for _ in range(3)]
    slot = 0
    for i in range(3):
        for j in range(i, 3):
            matrix[i][j] = sums[slot] + (1.0 if i == j else 0.0)
            matrix[j][i] = matrix[i][j]
            slot += 1
    answer = spd_solve(matrix, sums[6:9])
    rest = CAL_BASE - LANE
    for p in range(3):
        for par in range(2):
            first = par * CAL_BASE
            cal_ref[p:p + 1, first:first + LANE] = answer[p][2 * par:2 * par + 1, :]
            cal_ref[p:p + 1, first + LANE:first + CAL_BASE] = answer[p][2 * par + 1:2 * par + 2, :rest]


def on_device(
    prefit_resid, source_partials, attitude_partials, spline_position, calib_partials, obs_source,
    block_count, obs_range, obs_knot, obs_unit, given_inverse, knot_decay,
):
    update, packed = obs_call(
        block_count, prefit_resid, source_partials, attitude_partials, spline_position,
        calib_partials, obs_source, obs_range, obs_knot, obs_unit,
    )
    own = jnp.sum(lax.all_to_all(packed, "wide", 0, 0), axis=0)
    others = [
        lax.ppermute(own, "narrow", [(i, (i + shift) % 4) for i in range(4)]) for shift in (1, 2, 3)
    ]
    group = lax.axis_index("narrow").reshape(1).astype(jnp.int32)
    scalar = pl.BlockSpec(memory_space=pltpu.SMEM)
    vector = pl.BlockSpec(memory_space=pltpu.VMEM)
    small = jax.ShapeDtypeStruct((4, 256), F32)
    send, mul, add = pl.pallas_call(
        join_kernel,
        in_specs=[scalar] + [vector] * 6,
        out_shape=[jax.ShapeDtypeStruct((32, 8, LANE), F32), small, small],
        scratch_shapes=[pltpu.VMEM((16, LANE), F32)],
        compiler_params=pltpu.CompilerParams(vmem_limit_bytes=16 * 1024 * 1024),
    )(group, own, *others, given_inverse, knot_decay)
    again = lax.all_to_all(send, "wide", 0, 0)
    mine = lax.axis_index("wide").reshape(1).astype(jnp.int32)
    att_update, cal_update = pl.pallas_call(
        last_kernel,
        in_specs=[scalar] + [vector] * 3,
        out_shape=[small, jax.ShapeDtypeStruct((3, 504), F32)],
        compiler_params=pltpu.CompilerParams(vmem_limit_bytes=16 * 1024 * 1024),
    )(mine, again, mul, add)
    return update, att_update, cal_update


def solution(mesh):
    both = ("wide", "narrow")
    placed = (
        P(both), P(None, both), P(None, both), P(both), P(None, both), P(both),
        P(both), P(both), P(both), P(both), P("wide", None, None), P(None, "wide"),
    )
    return jax.shard_map(
        on_device,
        mesh=mesh,
        in_specs=placed,
        out_specs=(P(None, both), P(None, "wide"), P(None, "narrow")),
        check_vma=False,
    )
```

time: 90 us -> 71.6 us (0.80)
  Pallas kernels: 48.7 us -> 29.5 us
    pallas_call x1, Pallas kernels: 46.4 us -> 27.1 us  [obs_call(): pl.pallas_call(obs_kernel, in_specs=[pl.BlockSpec(memory_space=pltpu.SMEM...]
where the time goes in v3:
time: 71.6 us; the launch traced here: 71.2 us
  Pallas kernels  29.5 us (41%)
  blocking collectives  19.4 us (27%)
  starting transfers between devices  10 us (14%)
  waiting for transfers between devices  9.42 us (13%)
  local copies, waits for them, and re-layouts  2.19 us (3%)
    pallas_call x1, Pallas kernels, obs_call(): pl.pallas_call(obs_kernel, in_specs=[pl.BlockSpec(memory_space=pltpu.SMEM...  27.1 us
    all_to_all x1, blocking collectives, on_device(): own = jnp.sum(lax.all_to_all(packed, 'wide', 0, 0), axis=0)  19.4 us
    all_to_all x1, waiting for transfers between devices, on_device(): again = lax.all_to_all(send, 'wide', 0, 0)  7.81 us
    all_to_all x1, starting transfers between devices, on_device(): again = lax.all_to_all(send, 'wide', 0, 0)  5.1 us
    ppermute x3, starting transfers between devices, on_device(): lax.ppermute(own, 'narrow', [(i, (i + shift) % 4) for i in range(4)])  4.92 us
    unnamed x4, local copies, waits for them, and re-layouts  2.19 us
    pallas_call x1, Pallas kernels, on_device(): pl.pallas_call(join_kernel, in_specs=[scalar] + [vector] * 6, out_shape=[...  1.63 us
    ppermute x3, waiting for transfers between devices, on_device(): lax.ppermute(own, 'narrow', [(i, (i + shift) % 4) for i in range(4)])  1.61 us
  transfers between devices with their start and end apart: 4, of which 3 were waited for; matrix products, arithmetic and copies ran while one was open for 0% of the time, Pallas kernels for 0%

profile of v3, /device:TPU:1, one launch (start us, length us, event | category | flops | bytes accessed | tf_op | source)
XLA Modules:
  0.0 71.2 jit_solution(9690852662660228011)
XLA Ops:
  0.6 0.0 copy-start.1
  0.6 27.1 %shard_map.139 = (f32[5,8192]{1,0:T(8,128)}, f32[32,16,128]{2,1,0:T(8,128)}) custom-call(s32[64]{0:T(128)} %count_ref.1, f32[1,40960]{1,0:T(1,128)} %bitcast.8, f32[5,40960]{1,0:T(8,128)} %par_hbm.1, f32[4,40960]{1,0:T(4,128)} %att_hbm.1, f32[1,40960]{1,0:T(1,128)} %bitcast.9, f32[3,40960]{1,0:T(4,128)} %cal_hbm.1, s32[1,40960]{1,0:T(1,128)} %bitcast.10, ...), custom_call_target="tpu_custom_call" | custom-call | tf_op jit(solution)/shard_map/pallas_call | solution.py:307
  27.8 19.4 %all_to_all.10 = f32[32,16,128]{2,1,0:T(8,128)S(1)} all-to-all(f32[32,16,128]{2,1,0:T(8,128)} %get-tuple-element.11), channel_id=1, replica_groups=mesh['wide'=32,'narrow'=4] {'wide'}, dimensions={0} | all-to-all | bytes 524288 | tf_op jit(solution)/shard_map/all_to_all | solution.py:406
  47.2 1.3 %collective-permute-start = (f32[16,128]{1,0:T(8,128)S(1)}, f32[16,128]{1,0:T(8,128)S(1)}, u32[]{:S(2)}, u32[]{:S(2)}) collective-permute-start(f32[16,128]{1,0:T(8,128)S(1)} %reduce_sum.9.own_ref), channel_id=1, source_target_pairs={{0,1},{1,2},{2,3},{3,0},{4,5},{5,6},{6,7},{7,4},{8,9},{9,10},{10,1... | collective-permute-start | bytes 24584 | tf_op jit(solution)/shard_map/ppermute | solution.py:408
  48.5 2.4 %collective-permute-start.1 = (f32[16,128]{1,0:T(8,128)S(1)}, f32[16,128]{1,0:T(8,128)S(1)}, u32[]{:S(2)}, u32[]{:S(2)}) collective-permute-start(f32[16,128]{1,0:T(8,128)S(1)} %reduce_sum.9.own_ref), channel_id=1, source_target_pairs={{0,2},{1,3},{2,0},{3,1},{4,6},{5,7},{6,4},{7,5},{8,10},{9,11},{10,... | collective-permute-start | bytes 24584 | tf_op jit(solution)/shard_map/ppermute | solution.py:408
  50.9 1.2 %collective-permute-start.2 = (f32[16,128]{1,0:T(8,128)S(1)}, f32[16,128]{1,0:T(8,128)S(1)}, u32[]{:S(2)}, u32[]{:S(2)}) collective-permute-start(f32[16,128]{1,0:T(8,128)S(1)} %reduce_sum.9.own_ref), channel_id=1, source_target_pairs={{0,3},{1,0},{2,1},{3,2},{4,7},{5,4},{6,5},{7,6},{8,11},{9,8},{10,9... | collective-permute-start | bytes 24584 | tf_op jit(solution)/shard_map/ppermute | solution.py:408
  52.1 0.0 collective-permute-done.one_ref
  52.1 0.4 collective-permute-done.1.two_ref
  52.5 1.2 %collective-permute-done.2.three_ref = f32[16,128]{1,0:T(8,128)S(1)} collective-permute-done((f32[16,128]{1,0:T(8,128)S(1)}, f32[16,128]{1,0:T(8,128)S(1)}, u32[]{:S(2)}, u32[]{:S(2)}) %collective-permute-start.2) | collective-permute-done | bytes 8224 | tf_op jit(solution)/shard_map/ppermute | solution.py:408
  53.7 0.0 copy-done.1
  53.7 0.0 copy-start
  53.7 2.2 %copy-done = f32[1,1024,1024]{2,1,0:T(8,128)S(1)} copy-done((f32[1,1024,1024]{2,1,0:T(8,128)S(1)}, f32[1,1024,1024]{2,1,0:T(8,128)}, u32[]{:S(2)}) %copy-start) | copy-done | bytes 4194328
  55.9 1.6 %shard_map.140 = (f32[32,8,128]{2,1,0:T(8,128)}, f32[4,256]{1,0:T(4,128)S(1)}, f32[4,256]{1,0:T(4,128)S(1)}) custom-call(s32[1]{0:T(128)} %bitcast.7.group_ref, f32[16,128]{1,0:T(8,128)S(1)} %reduce_sum.9.own_ref, f32[16,128]{1,0:T(8,128)S(1)} %collective-permute-done.one_ref, f32[16,128]{1,0:T(8,128)S(1)} %collective-permute-done.1.two_ref, ...), custom_call_target="tpu_custom_call" | custom-call | tf_op jit(solution)/shard_map/pallas_call | solution.py:414
  57.5 5.1 %all-to-all-start.1 = ((f32[32,8,128]{2,1,0:T(8,128)}), f32[32,8,128]{2,1,0:T(8,128)S(1)}, u32[]{:S(2)}, u32[]{:S(2)}) async-start(f32[32,8,128]{2,1,0:T(8,128)} %get-tuple-element.12), calls=%async_computation.1 | async-start | bytes 262144 | tf_op jit(solution)/shard_map/all_to_all | solution.py:421
  62.7 7.8 %all-to-all-done.1.recv_ref = f32[32,8,128]{2,1,0:T(8,128)S(1)} async-done(((f32[32,8,128]{2,1,0:T(8,128)}), f32[32,8,128]{2,1,0:T(8,128)S(1)}, u32[]{:S(2)}, u32[]{:S(2)}) %all-to-all-start.1) | async-done | bytes 131104 | tf_op jit(solution)/shard_map/all_to_all | solution.py:421
  70.5 0.7 %shard_map.141 = (f32[4,256]{1,0:T(4,128)}, f32[3,504]{1,0:T(4,128)}) custom-call(s32[1]{0:T(128)} %bitcast.6.mine_ref, f32[32,8,128]{2,1,0:T(8,128)S(1)} %all-to-all-done.1.recv_ref, f32[4,256]{1,0:T(4,128)S(1)} %get-tuple-element.13.mul_ref, f32[4,256]{1,0:T(4,128)S(1)} %get-tuple-element.14.add_ref), custom_call_target="tpu_custom_call" | custom-call | tf_op jit(solution)/shard_map/pallas_call | solution.py:423
  (1 shorter events, 0.0 us)
Async XLA Ops:
  0.6 53.1 %copy-start.1 = (f32[4,256]{1,0:T(4,128)S(1)}, f32[4,256]{1,0:T(4,128)}, u32[]{:S(2)}) copy-start(f32[4,256]{1,0:T(4,128)} %decay_ref.1) | copy-start | bytes 12292
  47.2 4.9 %collective-permute-start = (f32[16,128]{1,0:T(8,128)S(1)}, f32[16,128]{1,0:T(8,128)S(1)}, u32[]{:S(2)}, u32[]{:S(2)}) collective-permute-start(f32[16,128]{1,0:T(8,128)S(1)} %reduce_sum.9.own_ref), channel_id=1, source_target_pairs={{0,1},{1,2},{2,3},{3,0},{4,5},{5,6},{6,7},{7,4},{8,9},{9,10},{10,1... | collective-permute-start | bytes 24584 | tf_op jit(solution)/shard_map/ppermute | solution.py:408
  48.5 4.0 %collective-permute-start.1 = (f32[16,128]{1,0:T(8,128)S(1)}, f32[16,128]{1,0:T(8,128)S(1)}, u32[]{:S(2)}, u32[]{:S(2)}) collective-permute-start(f32[16,128]{1,0:T(8,128)S(1)} %reduce_sum.9.own_ref), channel_id=1, source_target_pairs={{0,2},{1,3},{2,0},{3,1},{4,6},{5,7},{6,4},{7,5},{8,10},{9,11},{10,... | collective-permute-start | bytes 24584 | tf_op jit(solution)/shard_map/ppermute | solution.py:408
  50.9 2.8 %collective-permute-start.2 = (f32[16,128]{1,0:T(8,128)S(1)}, f32[16,128]{1,0:T(8,128)S(1)}, u32[]{:S(2)}, u32[]{:S(2)}) collective-permute-start(f32[16,128]{1,0:T(8,128)S(1)} %reduce_sum.9.own_ref), channel_id=1, source_target_pairs={{0,3},{1,0},{2,1},{3,2},{4,7},{5,4},{6,5},{7,6},{8,11},{9,8},{10,9... | collective-permute-start | bytes 24584 | tf_op jit(solution)/shard_map/ppermute | solution.py:408
  53.7 2.2 %copy-start = (f32[1,1024,1024]{2,1,0:T(8,128)S(1)}, f32[1,1024,1024]{2,1,0:T(8,128)}, u32[]{:S(2)}) copy-start(f32[1,1024,1024]{2,1,0:T(8,128)} %inv_ref.1) | copy-start | bytes 12582916
  57.5 12.9 %all-to-all-start.1 = ((f32[32,8,128]{2,1,0:T(8,128)}), f32[32,8,128]{2,1,0:T(8,128)S(1)}, u32[]{:S(2)}, u32[]{:S(2)}) async-start(f32[32,8,128]{2,1,0:T(8,128)} %get-tuple-element.12), calls=%async_computation.1 | async-start | bytes 262144 | tf_op jit(solution)/shard_map/all_to_all | solution.py:421

commit v4 on v3

--- a/solution.py
+++ b/solution.py
@@ -7,15 +7,15 @@
 
 SRC_BLK = 128
 SLOT_BLK = 640
-CAL = 2016
 GRP = 8
-TURN = 16
+TURN = 32
+REST = 8
+SPAN = 4
 VMEM_OBS = 60 * 1024 * 1024
 LANE = 128
 ATT_BASE = 125
 ATT_HI = 68
 CAL_BASE = 252
-CAL_HI = 8
 F32 = jnp.float32
 BF16 = jnp.bfloat16
 
@@ -93,11 +93,12 @@
         return spot + lax.shift_right_logical(count + (LANE - 1), 7)
 
     used = lax.fori_loop(0, blocks, listing, 0)
-    for t in range(TURN):
+    for t in range(REST):
         start_s[used + t] = 0
         live_s[used + t] = 0
         block_s[used + t] = 0
-    turns = lax.div(used + (TURN - 1), TURN)
+    turns = lax.div(used, TURN)
+    rests = lax.div(used - turns * TURN + (REST - 1), REST)
 
     for copy in copies[:3]:
         copy.wait()
@@ -139,33 +140,43 @@
         return one_hot(wide16(ids).astype(BF16), 8), pieces
 
     def source_sums(accs):
-        def group_sums(group, _):
-            for pair in range(GRP // 2):
-                unit = pair % 2
-                block = group * GRP + 2 * pair
-                for t in range(tiles):
-                    left_hot, left = source_tile(block, t)
-                    right_hot, right = source_tile(block + 1, t)
-                    rows = [beside(piece, zero16) for piece in left_hot]
-                    rows += [beside(zero16, piece) for piece in right_hot]
-                    stage = t % 2 if unit == pair else (t + 1) % 2
-                    pltpu.matmul_push_rhs(jnp.concatenate(rows, axis=0), stage, unit, transpose=True)
-                    for d in range(2):
-                        for k in range(3):
-                            pltpu.matmul_acc_lhs(
-                                accs[pair][d], beside(left[d][k], right[d][k]), stage if d + k == 0 else None
-                            )
-            for pair in range(GRP // 2):
+        def spend_pair(group, pair, mine):
+            unit = pair % 2
+            block = group * GRP + 2 * pair
+            for t in range(tiles):
+                left_hot, left = source_tile(block, t)
+                right_hot, right = source_tile(block + 1, t)
+                rows = [beside(piece, zero16) for piece in left_hot]
+                rows += [beside(zero16, piece) for piece in right_hot]
+                stage = t % 2 if unit == pair else (t + 1) % 2
+                pltpu.matmul_push_rhs(jnp.concatenate(rows, axis=0), stage, unit, transpose=True)
                 for d in range(2):
-                    sums = pltpu.matmul_pop(accs[pair][d])
-                    for side in range(2):
-                        sums_s[group, 16 * d:16 * d + 16, 2 * pair + side, :] = sums[:, side * LANE:(side + 1) * LANE]
+                    for k in range(3):
+                        pltpu.matmul_acc_lhs(mine[d], beside(left[d][k], right[d][k]), stage if d + k == 0 else None)
+
+        def keep_pair(group, pair, mine):
+            for d in range(2):
+                sums = pltpu.matmul_pop(mine[d])
+                for side in range(2):
+                    sums_s[group, 16 * d:16 * d + 16, 2 * pair + side, :] = sums[:, side * LANE:(side + 1) * LANE]
+
+        def group_sums(turn_at, _):
+            for part in range(SPAN):
+                for pair in range(GRP // 2):
+                    spend_pair(turn_at * SPAN + part, pair, accs[part][pair])
+            for part in range(SPAN):
+                for pair in range(GRP // 2):
+                    keep_pair(turn_at * SPAN + part, pair, accs[part][pair])
             return 0
 
-        lax.fori_loop(0, blocks // GRP, group_sums, 0)
+        lax.fori_loop(0, blocks // (GRP * SPAN), group_sums, 0)
 
     pl.run_scoped(
-        source_sums, [[pltpu.ACC(pair % 2)((16, 256), F32) for _ in range(2)] for pair in range(GRP // 2)]
+        source_sums,
+        [
+            [[pltpu.ACC(pair % 2)((16, 256), F32) for _ in range(2)] for pair in range(GRP // 2)]
+            for _ in range(SPAN)
+        ],
     )
 
     matrix = [[None] * 5 for _ in range(5)]
@@ -262,7 +273,13 @@
                 spend(turn_at * TURN + 2 * part, part % 2)
             return 0
 
+        def rest(rest_at, _):
+            for part in range(REST // 2):
+                spend(turns * TURN + rest_at * REST + 2 * part, part % 2)
+            return 0
+
         lax.fori_loop(0, turns, turn, 0)
+        lax.fori_loop(0, rests, rest, 0)
         for t in range(ATT_HI // 4):
             parts = [pltpu.matmul_pop(att_accs[unit][2 * t + k]) for unit in range(2) for k in range(2)]
             att_acc[t * 16:(t + 1) * 16, :] = (parts[0] + parts[1]) + (parts[2] + parts[3])
@@ -329,7 +346,12 @@
     )(block_count, flat(prefit), partials, attitude, flat(position), calib, flat(source), flat(rng), flat(knot), flat(unit))
 
 
-def join_kernel(group_ref, own_ref, one_ref, two_ref, three_ref, inv_ref, decay_ref, send_ref, mul_ref, add_ref, rows_s):
+def join_kernel(group_ref, own_ref, one_ref, two_ref, three_ref, inv_hbm, decay_ref, send_ref, mul_ref, add_ref, rows_s, inv_ref, sems):
+    copies = []
+    for spot in range(8):
+        rows = pl.ds((spot % 4) * 256 + (spot // 4) * LANE, LANE)
+        copies.append(pltpu.make_async_copy(inv_hbm.at[0, rows, :], inv_ref.at[rows, :], sems.at[spot]))
+        copies[-1].start()
     total = own_ref[...] + one_ref[...] + two_ref[...] + three_ref[...]
     rows_s[...] = total
     group = group_ref[0]
@@ -339,8 +361,9 @@
             spot = half * 4 + c
             col = jnp.broadcast_to(total[spot:spot + 1, :], (LANE, LANE)).T
             first = c * 256 + half * LANE
+            copies[spot].wait()
             for s in range(LANE // 8):
-                line = inv_ref[0, first + s * 8:first + s * 8 + 8, :]
+                line = inv_ref[first + s * 8:first + s * 8 + 8, :]
                 acc = acc + line * jnp.concatenate([col[s * 8:s * 8 + 8, :]] * 8, axis=1)
     flat = jnp.sum(acc, axis=0, keepdims=True)
     solved = jnp.concatenate([flat[:, c * 256:(c + 1) * 256] for c in range(4)], axis=0)
@@ -413,10 +436,14 @@
     small = jax.ShapeDtypeStruct((4, 256), F32)
     send, mul, add = pl.pallas_call(
         join_kernel,
-        in_specs=[scalar] + [vector] * 6,
+        in_specs=[scalar] + [vector] * 4 + [pl.BlockSpec(memory_space=pl.ANY), vector],
         out_shape=[jax.ShapeDtypeStruct((32, 8, LANE), F32), small, small],
-        scratch_shapes=[pltpu.VMEM((16, LANE), F32)],
-        compiler_params=pltpu.CompilerParams(vmem_limit_bytes=16 * 1024 * 1024),
+        scratch_shapes=[
+            pltpu.VMEM((16, LANE), F32),
+            pltpu.VMEM(given_inverse.shape[1:], F32),
+            pltpu.SemaphoreType.DMA((8,)),
+        ],
+        compiler_params=pltpu.CompilerParams(vmem_limit_bytes=52 * 1024 * 1024),
     )(group, own, *others, given_inverse, knot_decay)
     again = lax.all_to_all(send, "wide", 0, 0)
     mine = lax.axis_index("wide").reshape(1).astype(jnp.int32)

time: 71.6 us -> 68.6 us (0.958)
  local copies, waits for them, and re-layouts: 2.19 us -> 0.01 us
  waiting for transfers between devices: 9.42 us -> 8.63 us
    unnamed x4 -> x2, local copies, waits for them, and re-layouts: 2.19 us -> 0.01 us
    pallas_call x1, Pallas kernels: 27.1 us -> 25.2 us  [obs_call(): pl.pallas_call(obs_kernel, in_specs=[pl.BlockSpec(memory_space=pltpu.SMEM...]
    pallas_call x1, Pallas kernels: 1.63 us -> 3.51 us  [on_device(): pl.pallas_call(join_kernel, in_specs=[scalar] + [vector] * 4 + [pl.BlockS...]
    ppermute x3, waiting for transfers between devices: 1.61 us -> 0.82 us  [on_device(): lax.ppermute(own, 'narrow', [(i, (i + shift) % 4) for i in range(4)])]
  transfers between devices with their start and end apart: 4 -> 4, of which waited for: 3 -> 2; matrix products, arithmetic and copies ran while one was open for 0% -> 0% of each run, Pallas kernels for 0% -> 0%
where the time goes in v4:
time: 68.6 us; the launch traced here: 68.4 us
  Pallas kernels  29.4 us (43%)
  blocking collectives  19 us (28%)
  starting transfers between devices  10.6 us (15%)
  waiting for transfers between devices  8.63 us (13%)
    pallas_call x1, Pallas kernels, obs_call(): pl.pallas_call(obs_kernel, in_specs=[pl.BlockSpec(memory_space=pltpu.SMEM...  25.2 us
    all_to_all x1, blocking collectives, on_device(): own = jnp.sum(lax.all_to_all(packed, 'wide', 0, 0), axis=0)  19 us
    all_to_all x1, waiting for transfers between devices, on_device(): again = lax.all_to_all(send, 'wide', 0, 0)  7.81 us
    ppermute x3, starting transfers between devices, on_device(): lax.ppermute(own, 'narrow', [(i, (i + shift) % 4) for i in range(4)])  5.54 us
    all_to_all x1, starting transfers between devices, on_device(): again = lax.all_to_all(send, 'wide', 0, 0)  5.09 us
    pallas_call x1, Pallas kernels, on_device(): pl.pallas_call(join_kernel, in_specs=[scalar] + [vector] * 4 + [pl.BlockS...  3.51 us
  transfers between devices with their start and end apart: 4, of which 2 were waited for; matrix products, arithmetic and copies ran while one was open for 0% of the time, Pallas kernels for 0%

profile of v4, /device:TPU:1, one launch (start us, length us, event | category | flops | bytes accessed | tf_op | source)
XLA Modules:
  0.0 68.4 jit_solution(977014688217185473)
XLA Ops:
  0.6 0.0 copy-start
  0.6 25.2 %shard_map.139 = (f32[5,8192]{1,0:T(8,128)}, f32[32,16,128]{2,1,0:T(8,128)}) custom-call(s32[64]{0:T(128)} %count_ref.1, f32[1,40960]{1,0:T(1,128)} %bitcast.8, f32[5,40960]{1,0:T(8,128)} %par_hbm.1, f32[4,40960]{1,0:T(4,128)} %att_hbm.1, f32[1,40960]{1,0:T(1,128)} %bitcast.9, f32[3,40960]{1,0:T(4,128)} %cal_hbm.1, s32[1,40960]{1,0:T(1,128)} %bitcast.10, ...), custom_call_target="tpu_custom_call" | custom-call | tf_op jit(solution)/shard_map/pallas_call | solution.py:324
  25.8 19.0 %all_to_all.10 = f32[32,16,128]{2,1,0:T(8,128)S(1)} all-to-all(f32[32,16,128]{2,1,0:T(8,128)} %get-tuple-element.11), channel_id=1, replica_groups=mesh['wide'=32,'narrow'=4] {'wide'}, dimensions={0} | all-to-all | bytes 524288 | tf_op jit(solution)/shard_map/all_to_all | solution.py:429
  44.9 1.2 %collective-permute-start = (f32[16,128]{1,0:T(8,128)S(1)}, f32[16,128]{1,0:T(8,128)S(1)}, u32[]{:S(2)}, u32[]{:S(2)}) collective-permute-start(f32[16,128]{1,0:T(8,128)S(1)} %reduce_sum.9.own_ref), channel_id=1, source_target_pairs={{0,1},{1,2},{2,3},{3,0},{4,5},{5,6},{6,7},{7,4},{8,9},{9,10},{10,1... | collective-permute-start | bytes 24584 | tf_op jit(solution)/shard_map/ppermute | solution.py:431
  46.1 2.4 %collective-permute-start.1 = (f32[16,128]{1,0:T(8,128)S(1)}, f32[16,128]{1,0:T(8,128)S(1)}, u32[]{:S(2)}, u32[]{:S(2)}) collective-permute-start(f32[16,128]{1,0:T(8,128)S(1)} %reduce_sum.9.own_ref), channel_id=1, source_target_pairs={{0,2},{1,3},{2,0},{3,1},{4,6},{5,7},{6,4},{7,5},{8,10},{9,11},{10,... | collective-permute-start | bytes 24584 | tf_op jit(solution)/shard_map/ppermute | solution.py:431
  48.4 2.0 %collective-permute-start.2 = (f32[16,128]{1,0:T(8,128)S(1)}, f32[16,128]{1,0:T(8,128)S(1)}, u32[]{:S(2)}, u32[]{:S(2)}) collective-permute-start(f32[16,128]{1,0:T(8,128)S(1)} %reduce_sum.9.own_ref), channel_id=1, source_target_pairs={{0,3},{1,0},{2,1},{3,2},{4,7},{5,4},{6,5},{7,6},{8,11},{9,8},{10,9... | collective-permute-start | bytes 24584 | tf_op jit(solution)/shard_map/ppermute | solution.py:431
  50.4 0.0 collective-permute-done.one_ref
  50.4 0.0 collective-permute-done.1.two_ref
  50.4 0.8 %collective-permute-done.2.three_ref = f32[16,128]{1,0:T(8,128)S(1)} collective-permute-done((f32[16,128]{1,0:T(8,128)S(1)}, f32[16,128]{1,0:T(8,128)S(1)}, u32[]{:S(2)}, u32[]{:S(2)}) %collective-permute-start.2) | collective-permute-done | bytes 8224 | tf_op jit(solution)/shard_map/ppermute | solution.py:431
  51.2 0.0 copy-done
  51.2 3.5 %shard_map.140 = (f32[32,8,128]{2,1,0:T(8,128)}, f32[4,256]{1,0:T(4,128)S(1)}, f32[4,256]{1,0:T(4,128)S(1)}) custom-call(s32[1]{0:T(128)} %bitcast.7.group_ref, f32[16,128]{1,0:T(8,128)S(1)} %reduce_sum.9.own_ref, f32[16,128]{1,0:T(8,128)S(1)} %collective-permute-done.one_ref, f32[16,128]{1,0:T(8,128)S(1)} %collective-permute-done.1.two_ref, ...), custom_call_target="tpu_custom_call" | custom-call | tf_op jit(solution)/shard_map/pallas_call | solution.py:437
  54.8 5.1 %all-to-all-start.1 = ((f32[32,8,128]{2,1,0:T(8,128)}), f32[32,8,128]{2,1,0:T(8,128)S(1)}, u32[]{:S(2)}, u32[]{:S(2)}) async-start(f32[32,8,128]{2,1,0:T(8,128)} %get-tuple-element.12), calls=%async_computation.1 | async-start | bytes 262144 | tf_op jit(solution)/shard_map/all_to_all | solution.py:448
  59.9 7.8 %all-to-all-done.1.recv_ref = f32[32,8,128]{2,1,0:T(8,128)S(1)} async-done(((f32[32,8,128]{2,1,0:T(8,128)}), f32[32,8,128]{2,1,0:T(8,128)S(1)}, u32[]{:S(2)}, u32[]{:S(2)}) %all-to-all-start.1) | async-done | bytes 131104 | tf_op jit(solution)/shard_map/all_to_all | solution.py:448
  67.7 0.7 %shard_map.141 = (f32[4,256]{1,0:T(4,128)}, f32[3,504]{1,0:T(4,128)}) custom-call(s32[1]{0:T(128)} %bitcast.6.mine_ref, f32[32,8,128]{2,1,0:T(8,128)S(1)} %all-to-all-done.1.recv_ref, f32[4,256]{1,0:T(4,128)S(1)} %get-tuple-element.13.mul_ref, f32[4,256]{1,0:T(4,128)S(1)} %get-tuple-element.14.add_ref), custom_call_target="tpu_custom_call" | custom-call | tf_op jit(solution)/shard_map/pallas_call | solution.py:450
  (1 shorter events, 0.0 us)
Async XLA Ops:
  0.6 50.6 %copy-start = (f32[4,256]{1,0:T(4,128)S(1)}, f32[4,256]{1,0:T(4,128)}, u32[]{:S(2)}) copy-start(f32[4,256]{1,0:T(4,128)} %decay_ref.1) | copy-start | bytes 12292
  44.9 5.5 %collective-permute-start = (f32[16,128]{1,0:T(8,128)S(1)}, f32[16,128]{1,0:T(8,128)S(1)}, u32[]{:S(2)}, u32[]{:S(2)}) collective-permute-start(f32[16,128]{1,0:T(8,128)S(1)} %reduce_sum.9.own_ref), channel_id=1, source_target_pairs={{0,1},{1,2},{2,3},{3,0},{4,5},{5,6},{6,7},{7,4},{8,9},{9,10},{10,1... | collective-permute-start | bytes 24584 | tf_op jit(solution)/shard_map/ppermute | solution.py:431
  46.1 4.3 %collective-permute-start.1 = (f32[16,128]{1,0:T(8,128)S(1)}, f32[16,128]{1,0:T(8,128)S(1)}, u32[]{:S(2)}, u32[]{:S(2)}) collective-permute-start(f32[16,128]{1,0:T(8,128)S(1)} %reduce_sum.9.own_ref), channel_id=1, source_target_pairs={{0,2},{1,3},{2,0},{3,1},{4,6},{5,7},{6,4},{7,5},{8,10},{9,11},{10,... | collective-permute-start | bytes 24584 | tf_op jit(solution)/shard_map/ppermute | solution.py:431
  48.4 2.8 %collective-permute-start.2 = (f32[16,128]{1,0:T(8,128)S(1)}, f32[16,128]{1,0:T(8,128)S(1)}, u32[]{:S(2)}, u32[]{:S(2)}) collective-permute-start(f32[16,128]{1,0:T(8,128)S(1)} %reduce_sum.9.own_ref), channel_id=1, source_target_pairs={{0,3},{1,0},{2,1},{3,2},{4,7},{5,4},{6,5},{7,6},{8,11},{9,8},{10,9... | collective-permute-start | bytes 24584 | tf_op jit(solution)/shard_map/ppermute | solution.py:431
  54.8 12.9 %all-to-all-start.1 = ((f32[32,8,128]{2,1,0:T(8,128)}), f32[32,8,128]{2,1,0:T(8,128)S(1)}, u32[]{:S(2)}, u32[]{:S(2)}) async-start(f32[32,8,128]{2,1,0:T(8,128)} %get-tuple-element.12), calls=%async_computation.1 | async-start | bytes 262144 | tf_op jit(solution)/shard_map/all_to_all | solution.py:448

commit v5 on v4

--- a/solution.py
+++ b/solution.py
@@ -11,7 +11,7 @@
 TURN = 32
 REST = 8
 SPAN = 4
-VMEM_OBS = 60 * 1024 * 1024
+VMEM_OBS = 16 * 1024 * 1024
 LANE = 128
 ATT_BASE = 125
 ATT_HI = 68
@@ -318,12 +318,13 @@
 def obs_call(block_count, prefit, partials, attitude, position, calib, source, rng, knot, unit):
     blocks = block_count.shape[0]
     count = prefit.shape[0]
-    flat = lambda value: value.reshape(1, -1)
+    pin = lambda value: pltpu.with_memory_space_constraint(value, pltpu.HBM)
+    flat = lambda value: pin(value.reshape(1, -1))
     row = lambda kind: pltpu.VMEM((1, count), kind)
     listed = pltpu.SMEM((count // LANE + TURN + 8,), jnp.int32)
     return pl.pallas_call(
         obs_kernel,
-        in_specs=[pl.BlockSpec(memory_space=pltpu.SMEM)] + [pl.BlockSpec(memory_space=pl.ANY)] * 9,
+        in_specs=[pl.BlockSpec(memory_space=pltpu.SMEM)] + [pl.BlockSpec(memory_space=pltpu.HBM)] * 9,
         out_specs=[pl.BlockSpec(memory_space=pltpu.VMEM)] * 2,
         out_shape=[
             jax.ShapeDtypeStruct((5, blocks * SRC_BLK), F32),
@@ -343,7 +344,7 @@
             pltpu.SemaphoreType.DMA((9,)),
         ],
         compiler_params=pltpu.CompilerParams(vmem_limit_bytes=VMEM_OBS),
-    )(block_count, flat(prefit), partials, attitude, flat(position), calib, flat(source), flat(rng), flat(knot), flat(unit))
+    )(pin(block_count), flat(prefit), pin(partials), pin(attitude), flat(position), pin(calib), flat(source), flat(rng), flat(knot), flat(unit))
 
 
 def join_kernel(group_ref, own_ref, one_ref, two_ref, three_ref, inv_hbm, decay_ref, send_ref, mul_ref, add_ref, rows_s, inv_ref, sems):
@@ -436,15 +437,15 @@
     small = jax.ShapeDtypeStruct((4, 256), F32)
     send, mul, add = pl.pallas_call(
         join_kernel,
-        in_specs=[scalar] + [vector] * 4 + [pl.BlockSpec(memory_space=pl.ANY), vector],
+        in_specs=[scalar] + [vector] * 4 + [pl.BlockSpec(memory_space=pltpu.HBM), vector],
         out_shape=[jax.ShapeDtypeStruct((32, 8, LANE), F32), small, small],
         scratch_shapes=[
             pltpu.VMEM((16, LANE), F32),
             pltpu.VMEM(given_inverse.shape[1:], F32),
             pltpu.SemaphoreType.DMA((8,)),
         ],
-        compiler_params=pltpu.CompilerParams(vmem_limit_bytes=52 * 1024 * 1024),
-    )(group, own, *others, given_inverse, knot_decay)
+        compiler_params=pltpu.CompilerParams(vmem_limit_bytes=16 * 1024 * 1024),
+    )(group, own, *others, pltpu.with_memory_space_constraint(given_inverse, pltpu.HBM), knot_decay)
     again = lax.all_to_all(send, "wide", 0, 0)
     mine = lax.axis_index("wide").reshape(1).astype(jnp.int32)
     att_update, cal_update = pl.pallas_call(

time: 68.6 us -> 68.4 us (level)
  no operation moved by 1% of the time
where the time goes in v5:
time: 68.4 us; the launch traced here: 68 us
  Pallas kernels  29.3 us (43%)
  blocking collectives  18.7 us (27%)
  starting transfers between devices  10.7 us (16%)
  waiting for transfers between devices  8.61 us (13%)
    pallas_call x1, Pallas kernels, obs_call(): pl.pallas_call(obs_kernel, in_specs=[pl.BlockSpec(memory_space=pltpu.SMEM...  25 us
    all_to_all x1, blocking collectives, on_device(): own = jnp.sum(lax.all_to_all(packed, 'wide', 0, 0), axis=0)  18.7 us
    all_to_all x1, waiting for transfers between devices, on_device(): again = lax.all_to_all(send, 'wide', 0, 0)  7.81 us
    all_to_all x1, starting transfers between devices, on_device(): again = lax.all_to_all(send, 'wide', 0, 0)  5.41 us
    ppermute x3, starting transfers between devices, on_device(): lax.ppermute(own, 'narrow', [(i, (i + shift) % 4) for i in range(4)])  5.29 us
    pallas_call x1, Pallas kernels, on_device(): pl.pallas_call(join_kernel, in_specs=[scalar] + [vector] * 4 + [pl.BlockS...  3.51 us
  transfers between devices with their start and end apart: 4, of which 2 were waited for; matrix products, arithmetic and copies ran while one was open for 0% of the time, Pallas kernels for 0%

profile of v5, /device:TPU:1, one launch (start us, length us, event | category | flops | bytes accessed | tf_op | source)
XLA Modules:
  0.0 68.0 jit_solution(10453429612413646208)
XLA Ops:
  0.6 0.0 copy-start
  0.6 25.0 %shard_map.139 = (f32[5,8192]{1,0:T(8,128)}, f32[32,16,128]{2,1,0:T(8,128)S(1)}) custom-call(s32[64]{0:T(128)} %count_ref.1, f32[1,40960]{1,0:T(1,128)} %bitcast.8, f32[5,40960]{1,0:T(8,128)} %par_hbm.1, f32[4,40960]{1,0:T(4,128)} %att_hbm.1, f32[1,40960]{1,0:T(1,128)} %bitcast.9, f32[3,40960]{1,0:T(4,128)} %cal_hbm.1, s32[1,40960]{1,0:T(1,128)} %bitcast.10, ...), custom_call_target="tpu_custom_call" | custom-call | tf_op jit(solution)/shard_map/pallas_call | solution.py:325
  25.7 18.7 %all_to_all.10 = f32[32,16,128]{2,1,0:T(8,128)S(1)} all-to-all(f32[32,16,128]{2,1,0:T(8,128)S(1)} %get-tuple-element.11), channel_id=1, replica_groups=mesh['wide'=32,'narrow'=4] {'wide'}, dimensions={0} | all-to-all | bytes 524288 | tf_op jit(solution)/shard_map/all_to_all | solution.py:430
  44.5 0.8 %collective-permute-start = (f32[16,128]{1,0:T(8,128)S(1)}, f32[16,128]{1,0:T(8,128)S(1)}, u32[]{:S(2)}, u32[]{:S(2)}) collective-permute-start(f32[16,128]{1,0:T(8,128)S(1)} %reduce_sum.9.own_ref), channel_id=1, source_target_pairs={{0,1},{1,2},{2,3},{3,0},{4,5},{5,6},{6,7},{7,4},{8,9},{9,10},{10,1... | collective-permute-start | bytes 24584 | tf_op jit(solution)/shard_map/ppermute | solution.py:432
  45.3 2.8 %collective-permute-start.1 = (f32[16,128]{1,0:T(8,128)S(1)}, f32[16,128]{1,0:T(8,128)S(1)}, u32[]{:S(2)}, u32[]{:S(2)}) collective-permute-start(f32[16,128]{1,0:T(8,128)S(1)} %reduce_sum.9.own_ref), channel_id=1, source_target_pairs={{0,2},{1,3},{2,0},{3,1},{4,6},{5,7},{6,4},{7,5},{8,10},{9,11},{10,... | collective-permute-start | bytes 24584 | tf_op jit(solution)/shard_map/ppermute | solution.py:432
  48.0 1.7 %collective-permute-start.2 = (f32[16,128]{1,0:T(8,128)S(1)}, f32[16,128]{1,0:T(8,128)S(1)}, u32[]{:S(2)}, u32[]{:S(2)}) collective-permute-start(f32[16,128]{1,0:T(8,128)S(1)} %reduce_sum.9.own_ref), channel_id=1, source_target_pairs={{0,3},{1,0},{2,1},{3,2},{4,7},{5,4},{6,5},{7,6},{8,11},{9,8},{10,9... | collective-permute-start | bytes 24584 | tf_op jit(solution)/shard_map/ppermute | solution.py:432
  49.7 0.0 collective-permute-done.one_ref
  49.8 0.0 collective-permute-done.1.two_ref
  49.8 0.8 %collective-permute-done.2.three_ref = f32[16,128]{1,0:T(8,128)S(1)} collective-permute-done((f32[16,128]{1,0:T(8,128)S(1)}, f32[16,128]{1,0:T(8,128)S(1)}, u32[]{:S(2)}, u32[]{:S(2)}) %collective-permute-start.2) | collective-permute-done | bytes 8224 | tf_op jit(solution)/shard_map/ppermute | solution.py:432
  50.5 0.0 copy-done
  50.5 3.5 %shard_map.140 = (f32[32,8,128]{2,1,0:T(8,128)}, f32[4,256]{1,0:T(4,128)S(1)}, f32[4,256]{1,0:T(4,128)S(1)}) custom-call(s32[1]{0:T(128)} %bitcast.7.group_ref, f32[16,128]{1,0:T(8,128)S(1)} %reduce_sum.9.own_ref, f32[16,128]{1,0:T(8,128)S(1)} %collective-permute-done.one_ref, f32[16,128]{1,0:T(8,128)S(1)} %collective-permute-done.1.two_ref, ...), custom_call_target="tpu_custom_call" | custom-call | tf_op jit(solution)/shard_map/pallas_call | solution.py:438
  54.1 5.4 %all-to-all-start.1 = ((f32[32,8,128]{2,1,0:T(8,128)}), f32[32,8,128]{2,1,0:T(8,128)S(1)}, u32[]{:S(2)}, u32[]{:S(2)}) async-start(f32[32,8,128]{2,1,0:T(8,128)} %get-tuple-element.12), calls=%async_computation.1 | async-start | bytes 262144 | tf_op jit(solution)/shard_map/all_to_all | solution.py:449
  59.5 7.8 %all-to-all-done.1.recv_ref = f32[32,8,128]{2,1,0:T(8,128)S(1)} async-done(((f32[32,8,128]{2,1,0:T(8,128)}), f32[32,8,128]{2,1,0:T(8,128)S(1)}, u32[]{:S(2)}, u32[]{:S(2)}) %all-to-all-start.1) | async-done | bytes 131104 | tf_op jit(solution)/shard_map/all_to_all | solution.py:449
  67.3 0.7 %shard_map.141 = (f32[4,256]{1,0:T(4,128)}, f32[3,504]{1,0:T(4,128)}) custom-call(s32[1]{0:T(128)} %bitcast.6.mine_ref, f32[32,8,128]{2,1,0:T(8,128)S(1)} %all-to-all-done.1.recv_ref, f32[4,256]{1,0:T(4,128)S(1)} %get-tuple-element.13.mul_ref, f32[4,256]{1,0:T(4,128)S(1)} %get-tuple-element.14.add_ref), custom_call_target="tpu_custom_call" | custom-call | tf_op jit(solution)/shard_map/pallas_call | solution.py:451
  (1 shorter events, 0.0 us)
Async XLA Ops:
  0.6 49.9 %copy-start = (f32[4,256]{1,0:T(4,128)S(1)}, f32[4,256]{1,0:T(4,128)}, u32[]{:S(2)}) copy-start(f32[4,256]{1,0:T(4,128)} %decay_ref.1) | copy-start | bytes 12292
  44.5 5.3 %collective-permute-start = (f32[16,128]{1,0:T(8,128)S(1)}, f32[16,128]{1,0:T(8,128)S(1)}, u32[]{:S(2)}, u32[]{:S(2)}) collective-permute-start(f32[16,128]{1,0:T(8,128)S(1)} %reduce_sum.9.own_ref), channel_id=1, source_target_pairs={{0,1},{1,2},{2,3},{3,0},{4,5},{5,6},{6,7},{7,4},{8,9},{9,10},{10,1... | collective-permute-start | bytes 24584 | tf_op jit(solution)/shard_map/ppermute | solution.py:432
  45.3 4.5 %collective-permute-start.1 = (f32[16,128]{1,0:T(8,128)S(1)}, f32[16,128]{1,0:T(8,128)S(1)}, u32[]{:S(2)}, u32[]{:S(2)}) collective-permute-start(f32[16,128]{1,0:T(8,128)S(1)} %reduce_sum.9.own_ref), channel_id=1, source_target_pairs={{0,2},{1,3},{2,0},{3,1},{4,6},{5,7},{6,4},{7,5},{8,10},{9,11},{10,... | collective-permute-start | bytes 24584 | tf_op jit(solution)/shard_map/ppermute | solution.py:432
  48.0 2.5 %collective-permute-start.2 = (f32[16,128]{1,0:T(8,128)S(1)}, f32[16,128]{1,0:T(8,128)S(1)}, u32[]{:S(2)}, u32[]{:S(2)}) collective-permute-start(f32[16,128]{1,0:T(8,128)S(1)} %reduce_sum.9.own_ref), channel_id=1, source_target_pairs={{0,3},{1,0},{2,1},{3,2},{4,7},{5,4},{6,5},{7,6},{8,11},{9,8},{10,9... | collective-permute-start | bytes 24584 | tf_op jit(solution)/shard_map/ppermute | solution.py:432
  54.1 13.2 %all-to-all-start.1 = ((f32[32,8,128]{2,1,0:T(8,128)}), f32[32,8,128]{2,1,0:T(8,128)S(1)}, u32[]{:S(2)}, u32[]{:S(2)}) async-start(f32[32,8,128]{2,1,0:T(8,128)} %get-tuple-element.12), calls=%async_computation.1 | async-start | bytes 262144 | tf_op jit(solution)/shard_map/all_to_all | solution.py:449

commit v6 on v5

--- a/solution.py
+++ b/solution.py
@@ -347,12 +347,19 @@
     )(pin(block_count), flat(prefit), pin(partials), pin(attitude), flat(position), pin(calib), flat(source), flat(rng), flat(knot), flat(unit))
 
 
-def join_kernel(group_ref, own_ref, one_ref, two_ref, three_ref, inv_hbm, decay_ref, send_ref, mul_ref, add_ref, rows_s, inv_ref, sems):
+def hold_kernel(own_ref, inv_hbm, held_ref, sems):
     copies = []
-    for spot in range(8):
-        rows = pl.ds((spot % 4) * 256 + (spot // 4) * LANE, LANE)
-        copies.append(pltpu.make_async_copy(inv_hbm.at[0, rows, :], inv_ref.at[rows, :], sems.at[spot]))
+    for part in range(8):
+        rows = pl.ds(part * LANE, LANE)
+        copies.append(pltpu.make_async_copy(inv_hbm.at[:, rows, :], held_ref.at[:, rows, :], sems.at[part]))
         copies[-1].start()
+    for copy in copies:
+        copy.wait()
+
+
+def join_kernel(
+    group_ref, own_ref, one_ref, two_ref, three_ref, inv_ref, decay_ref, send_ref, mul_ref, add_ref, rows_s
+):
     total = own_ref[...] + one_ref[...] + two_ref[...] + three_ref[...]
     rows_s[...] = total
     group = group_ref[0]
@@ -362,9 +369,8 @@
             spot = half * 4 + c
             col = jnp.broadcast_to(total[spot:spot + 1, :], (LANE, LANE)).T
             first = c * 256 + half * LANE
-            copies[spot].wait()
             for s in range(LANE // 8):
-                line = inv_ref[first + s * 8:first + s * 8 + 8, :]
+                line = inv_ref[0, first + s * 8:first + s * 8 + 8, :]
                 acc = acc + line * jnp.concatenate([col[s * 8:s * 8 + 8, :]] * 8, axis=1)
     flat = jnp.sum(acc, axis=0, keepdims=True)
     solved = jnp.concatenate([flat[:, c * 256:(c + 1) * 256] for c in range(4)], axis=0)
@@ -431,21 +437,28 @@
     others = [
         lax.ppermute(own, "narrow", [(i, (i + shift) % 4) for i in range(4)]) for shift in (1, 2, 3)
     ]
+    held = pl.pallas_call(
+        hold_kernel,
+        in_specs=[pl.BlockSpec(memory_space=pltpu.VMEM), pl.BlockSpec(memory_space=pltpu.HBM)],
+        out_specs=pl.BlockSpec(memory_space=pltpu.VMEM),
+        out_shape=jax.ShapeDtypeStruct(given_inverse.shape, F32),
+        scratch_shapes=[pltpu.SemaphoreType.DMA((8,))],
+        compiler_params=pltpu.CompilerParams(vmem_limit_bytes=8 * 1024 * 1024),
+        cost_estimate=pl.CostEstimate(flops=0, bytes_accessed=8 * 1024 * 1024, transcendentals=0),
+    )(own, pltpu.with_memory_space_constraint(given_inverse, pltpu.HBM))
     group = lax.axis_index("narrow").reshape(1).astype(jnp.int32)
     scalar = pl.BlockSpec(memory_space=pltpu.SMEM)
     vector = pl.BlockSpec(memory_space=pltpu.VMEM)
     small = jax.ShapeDtypeStruct((4, 256), F32)
     send, mul, add = pl.pallas_call(
         join_kernel,
-        in_specs=[scalar] + [vector] * 4 + [pl.BlockSpec(memory_space=pltpu.HBM), vector],
+        in_specs=[scalar] + [vector] * 6,
         out_shape=[jax.ShapeDtypeStruct((32, 8, LANE), F32), small, small],
         scratch_shapes=[
             pltpu.VMEM((16, LANE), F32),
-            pltpu.VMEM(given_inverse.shape[1:], F32),
-            pltpu.SemaphoreType.DMA((8,)),
         ],
         compiler_params=pltpu.CompilerParams(vmem_limit_bytes=16 * 1024 * 1024),
-    )(group, own, *others, pltpu.with_memory_space_constraint(given_inverse, pltpu.HBM), knot_decay)
+    )(group, own, *others, held, knot_decay)
     again = lax.all_to_all(send, "wide", 0, 0)
     mine = lax.axis_index("wide").reshape(1).astype(jnp.int32)
     att_update, cal_update = pl.pallas_call(

time: 68.4 us -> 66.8 us (0.977)
  starting transfers between devices: 10.7 us -> 8.11 us
    ppermute x3, starting transfers between devices: 5.29 us -> 3.29 us  [on_device(): lax.ppermute(own, 'narrow', [(i, (i + shift) % 4) for i in range(4)])]
    pallas_call x1 -> x2, Pallas kernels: 3.51 us -> 3.85 us  [the longest x1 2.23 us: on_device(): pl.pallas_call(hold_kernel, in_specs=[pl.BlockSpec(memory_space=pltpu.VME...]
  transfers between devices with their start and end apart: 4 -> 4, of which waited for: 2 -> 2; matrix products, arithmetic and copies ran while one was open for 0% -> 0% of each run, Pallas kernels for 0% -> 3%
where the time goes in v6:
time: 66.8 us; the launch traced here: 66.5 us
  Pallas kernels  29.6 us (44%)
  blocking collectives  19.3 us (29%)
  waiting for transfers between devices  8.8 us (13%)
  starting transfers between devices  8.11 us (12%)
  between operations  0.69 us (1%)
    pallas_call x1, Pallas kernels, obs_call(): pl.pallas_call(obs_kernel, in_specs=[pl.BlockSpec(memory_space=pltpu.SMEM...  25 us
    all_to_all x1, blocking collectives, on_device(): own = jnp.sum(lax.all_to_all(packed, 'wide', 0, 0), axis=0)  19.3 us
    all_to_all x1, waiting for transfers between devices, on_device(): again = lax.all_to_all(send, 'wide', 0, 0)  7.81 us
    all_to_all x1, starting transfers between devices, on_device(): again = lax.all_to_all(send, 'wide', 0, 0)  4.83 us
    ppermute x3, starting transfers between devices, on_device(): lax.ppermute(own, 'narrow', [(i, (i + shift) % 4) for i in range(4)])  3.29 us
    pallas_call x1, Pallas kernels, on_device(): pl.pallas_call(hold_kernel, in_specs=[pl.BlockSpec(memory_space=pltpu.VME...  2.23 us
    pallas_call x1, Pallas kernels, on_device(): pl.pallas_call(join_kernel, in_specs=[scalar] + [vector] * 6, out_shape=[...  1.63 us
  transfers between devices with their start and end apart: 4, of which 2 were waited for; matrix products, arithmetic and copies ran while one was open for 0% of the time, Pallas kernels for 3%

profile of v6, /device:TPU:1, one launch (start us, length us, event | category | flops | bytes accessed | tf_op | source)
XLA Modules:
  0.0 66.5 jit_solution(15466067113616525603)
XLA Ops:
  0.6 25.0 %shard_map.139 = (f32[5,8192]{1,0:T(8,128)}, f32[32,16,128]{2,1,0:T(8,128)S(1)}) custom-call(s32[64]{0:T(128)} %count_ref.1, f32[1,40960]{1,0:T(1,128)} %bitcast.8, f32[5,40960]{1,0:T(8,128)} %par_hbm.1, f32[4,40960]{1,0:T(4,128)} %att_hbm.1, f32[1,40960]{1,0:T(1,128)} %bitcast.9, f32[3,40960]{1,0:T(4,128)} %cal_hbm.1, s32[1,40960]{1,0:T(1,128)} %bitcast.10, ...), custom_call_target="tpu_custom_call" | custom-call | tf_op jit(solution)/shard_map/pallas_call | solution.py:325
  25.6 19.3 %all_to_all.10 = f32[32,16,128]{2,1,0:T(8,128)S(1)} all-to-all(f32[32,16,128]{2,1,0:T(8,128)S(1)} %get-tuple-element.11), channel_id=1, replica_groups=mesh['wide'=32,'narrow'=4] {'wide'}, dimensions={0} | all-to-all | bytes 524288 | tf_op jit(solution)/shard_map/all_to_all | solution.py:436
  44.9 1.5 %collective-permute-start.2 = (f32[16,128]{1,0:T(8,128)S(1)}, f32[16,128]{1,0:T(8,128)S(1)}, u32[]{:S(2)}, u32[]{:S(2)}) collective-permute-start(f32[16,128]{1,0:T(8,128)S(1)} %reduce_sum.9.own_ref), channel_id=1, source_target_pairs={{0,3},{1,0},{2,1},{3,2},{4,7},{5,4},{6,5},{7,6},{8,11},{9,8},{10,9... | collective-permute-start | bytes 24584 | tf_op jit(solution)/shard_map/ppermute | solution.py:438
  46.4 1.0 %collective-permute-start.1 = (f32[16,128]{1,0:T(8,128)S(1)}, f32[16,128]{1,0:T(8,128)S(1)}, u32[]{:S(2)}, u32[]{:S(2)}) collective-permute-start(f32[16,128]{1,0:T(8,128)S(1)} %reduce_sum.9.own_ref), channel_id=1, source_target_pairs={{0,2},{1,3},{2,0},{3,1},{4,6},{5,7},{6,4},{7,5},{8,10},{9,11},{10,... | collective-permute-start | bytes 24584 | tf_op jit(solution)/shard_map/ppermute | solution.py:438
  47.4 0.8 %collective-permute-start = (f32[16,128]{1,0:T(8,128)S(1)}, f32[16,128]{1,0:T(8,128)S(1)}, u32[]{:S(2)}, u32[]{:S(2)}) collective-permute-start(f32[16,128]{1,0:T(8,128)S(1)} %reduce_sum.9.own_ref), channel_id=1, source_target_pairs={{0,1},{1,2},{2,3},{3,0},{4,5},{5,6},{6,7},{7,4},{8,9},{9,10},{10,1... | collective-permute-start | bytes 24584 | tf_op jit(solution)/shard_map/ppermute | solution.py:438
  48.2 0.0 copy-start
  48.2 2.2 %shard_map.140.inv_ref = f32[1,1024,1024]{2,1,0:T(8,128)S(1)} custom-call(f32[16,128]{1,0:T(8,128)S(1)} %reduce_sum.9.own_ref, f32[1,1024,1024]{2,1,0:T(8,128)} %inv_hbm.1), custom_call_target="tpu_custom_call" | custom-call | bytes 8388608 | tf_op jit(solution)/shard_map/pallas_call | solution.py:440
  50.4 0.0 collective-permute-done.2.three_ref
  50.4 0.0 collective-permute-done.1.two_ref
  50.5 1.0 %collective-permute-done.one_ref = f32[16,128]{1,0:T(8,128)S(1)} collective-permute-done((f32[16,128]{1,0:T(8,128)S(1)}, f32[16,128]{1,0:T(8,128)S(1)}, u32[]{:S(2)}, u32[]{:S(2)}) %collective-permute-start) | collective-permute-done | bytes 8224 | tf_op jit(solution)/shard_map/ppermute | solution.py:438
  51.4 0.0 copy-done
  51.4 1.6 %shard_map.141 = (f32[32,8,128]{2,1,0:T(8,128)}, f32[4,256]{1,0:T(4,128)S(1)}, f32[4,256]{1,0:T(4,128)S(1)}) custom-call(s32[1]{0:T(128)} %bitcast.7.group_ref, f32[16,128]{1,0:T(8,128)S(1)} %reduce_sum.9.own_ref, f32[16,128]{1,0:T(8,128)S(1)} %collective-permute-done.one_ref, f32[16,128]{1,0:T(8,128)S(1)} %collective-permute-done.1.two_ref, ...), custom_call_target="tpu_custom_call" | custom-call | tf_op jit(solution)/shard_map/pallas_call | solution.py:453
  53.1 4.8 %all-to-all-start.1 = ((f32[32,8,128]{2,1,0:T(8,128)}), f32[32,8,128]{2,1,0:T(8,128)S(1)}, u32[]{:S(2)}, u32[]{:S(2)}) async-start(f32[32,8,128]{2,1,0:T(8,128)} %get-tuple-element.12), calls=%async_computation.1 | async-start | bytes 262144 | tf_op jit(solution)/shard_map/all_to_all | solution.py:462
  57.9 7.8 %all-to-all-done.1.recv_ref = f32[32,8,128]{2,1,0:T(8,128)S(1)} async-done(((f32[32,8,128]{2,1,0:T(8,128)}), f32[32,8,128]{2,1,0:T(8,128)S(1)}, u32[]{:S(2)}, u32[]{:S(2)}) %all-to-all-start.1) | async-done | bytes 131104 | tf_op jit(solution)/shard_map/all_to_all | solution.py:462
  65.7 0.7 %shard_map.142 = (f32[4,256]{1,0:T(4,128)}, f32[3,504]{1,0:T(4,128)}) custom-call(s32[1]{0:T(128)} %bitcast.6.mine_ref, f32[32,8,128]{2,1,0:T(8,128)S(1)} %all-to-all-done.1.recv_ref, f32[4,256]{1,0:T(4,128)S(1)} %get-tuple-element.13.mul_ref, f32[4,256]{1,0:T(4,128)S(1)} %get-tuple-element.14.add_ref), custom_call_target="tpu_custom_call" | custom-call | tf_op jit(solution)/shard_map/pallas_call | solution.py:464
  (1 shorter events, 0.0 us)
Async XLA Ops:
  44.9 5.5 %collective-permute-start.2 = (f32[16,128]{1,0:T(8,128)S(1)}, f32[16,128]{1,0:T(8,128)S(1)}, u32[]{:S(2)}, u32[]{:S(2)}) collective-permute-start(f32[16,128]{1,0:T(8,128)S(1)} %reduce_sum.9.own_ref), channel_id=1, source_target_pairs={{0,3},{1,0},{2,1},{3,2},{4,7},{5,4},{6,5},{7,6},{8,11},{9,8},{10,9... | collective-permute-start | bytes 24584 | tf_op jit(solution)/shard_map/ppermute | solution.py:438
  46.4 4.1 %collective-permute-start.1 = (f32[16,128]{1,0:T(8,128)S(1)}, f32[16,128]{1,0:T(8,128)S(1)}, u32[]{:S(2)}, u32[]{:S(2)}) collective-permute-start(f32[16,128]{1,0:T(8,128)S(1)} %reduce_sum.9.own_ref), channel_id=1, source_target_pairs={{0,2},{1,3},{2,0},{3,1},{4,6},{5,7},{6,4},{7,5},{8,10},{9,11},{10,... | collective-permute-start | bytes 24584 | tf_op jit(solution)/shard_map/ppermute | solution.py:438
  47.4 4.0 %collective-permute-start = (f32[16,128]{1,0:T(8,128)S(1)}, f32[16,128]{1,0:T(8,128)S(1)}, u32[]{:S(2)}, u32[]{:S(2)}) collective-permute-start(f32[16,128]{1,0:T(8,128)S(1)} %reduce_sum.9.own_ref), channel_id=1, source_target_pairs={{0,1},{1,2},{2,3},{3,0},{4,5},{5,6},{6,7},{7,4},{8,9},{9,10},{10,1... | collective-permute-start | bytes 24584 | tf_op jit(solution)/shard_map/ppermute | solution.py:438
  48.2 3.2 %copy-start = (f32[4,256]{1,0:T(4,128)S(1)}, f32[4,256]{1,0:T(4,128)}, u32[]{:S(2)}) copy-start(f32[4,256]{1,0:T(4,128)} %decay_ref.1) | copy-start | bytes 12292
  53.1 12.6 %all-to-all-start.1 = ((f32[32,8,128]{2,1,0:T(8,128)}), f32[32,8,128]{2,1,0:T(8,128)S(1)}, u32[]{:S(2)}, u32[]{:S(2)}) async-start(f32[32,8,128]{2,1,0:T(8,128)} %get-tuple-element.12), calls=%async_computation.1 | async-start | bytes 262144 | tf_op jit(solution)/shard_map/all_to_all | solution.py:462

commit v7 on v6

--- a/solution.py
+++ b/solution.py
@@ -8,8 +8,8 @@
 SRC_BLK = 128
 SLOT_BLK = 640
 GRP = 8
-TURN = 32
-REST = 8
+TURN = 64
+REST = 4
 SPAN = 4
 VMEM_OBS = 16 * 1024 * 1024
 LANE = 128

time: 66.8 us -> 66.8 us (level)
  starting transfers between devices: 8.11 us -> 9.17 us
  blocking collectives: 19.3 us -> 18.5 us
  waiting for transfers between devices: 8.8 us -> 9.57 us
  Pallas kernels: 29.6 us -> 28.9 us
    ppermute x3, waiting for transfers between devices: 0.99 us -> 1.76 us  [on_device(): lax.ppermute(own, 'narrow', [(i, (i + shift) % 4) for i in range(4)])]
    ppermute x3, starting transfers between devices: 3.29 us -> 4.06 us  [on_device(): lax.ppermute(own, 'narrow', [(i, (i + shift) % 4) for i in range(4)])]
    all_to_all x1, blocking collectives: 19.3 us -> 18.5 us  [on_device(): own = jnp.sum(lax.all_to_all(packed, 'wide', 0, 0), axis=0)]
  transfers between devices with their start and end apart: 4 -> 4, of which waited for: 2 -> 3; matrix products, arithmetic and copies ran while one was open for 0% -> 0% of each run, Pallas kernels for 3% -> 3%
where the time goes in v7:
time: 66.8 us; the launch traced here: 66.9 us
  Pallas kernels  28.9 us (43%)
  blocking collectives  18.5 us (28%)
  waiting for transfers between devices  9.57 us (14%)
  starting transfers between devices  9.17 us (14%)
  between operations  0.68 us (1%)
    pallas_call x1, Pallas kernels, obs_call(): pl.pallas_call(obs_kernel, in_specs=[pl.BlockSpec(memory_space=pltpu.SMEM...  24.3 us
    all_to_all x1, blocking collectives, on_device(): own = jnp.sum(lax.all_to_all(packed, 'wide', 0, 0), axis=0)  18.5 us
    all_to_all x1, waiting for transfers between devices, on_device(): again = lax.all_to_all(send, 'wide', 0, 0)  7.81 us
    all_to_all x1, starting transfers between devices, on_device(): again = lax.all_to_all(send, 'wide', 0, 0)  5.11 us
    ppermute x3, starting transfers between devices, on_device(): lax.ppermute(own, 'narrow', [(i, (i + shift) % 4) for i in range(4)])  4.06 us
    pallas_call x1, Pallas kernels, on_device(): pl.pallas_call(hold_kernel, in_specs=[pl.BlockSpec(memory_space=pltpu.VME...  2.23 us
    ppermute x3, waiting for transfers between devices, on_device(): lax.ppermute(own, 'narrow', [(i, (i + shift) % 4) for i in range(4)])  1.76 us
    pallas_call x1, Pallas kernels, on_device(): pl.pallas_call(join_kernel, in_specs=[scalar] + [vector] * 6, out_shape=[...  1.63 us
  transfers between devices with their start and end apart: 4, of which 3 were waited for; matrix products, arithmetic and copies ran while one was open for 0% of the time, Pallas kernels for 3%

profile of v7, /device:TPU:1, one launch (start us, length us, event | category | flops | bytes accessed | tf_op | source)
XLA Modules:
  0.0 66.9 jit_solution(16757330604005386701)
XLA Ops:
  0.6 24.3 %shard_map.139 = (f32[5,8192]{1,0:T(8,128)}, f32[32,16,128]{2,1,0:T(8,128)S(1)}) custom-call(s32[64]{0:T(128)} %count_ref.1, f32[1,40960]{1,0:T(1,128)} %bitcast.8, f32[5,40960]{1,0:T(8,128)} %par_hbm.1, f32[4,40960]{1,0:T(4,128)} %att_hbm.1, f32[1,40960]{1,0:T(1,128)} %bitcast.9, f32[3,40960]{1,0:T(4,128)} %cal_hbm.1, s32[1,40960]{1,0:T(1,128)} %bitcast.10, ...), custom_call_target="tpu_custom_call" | custom-call | tf_op jit(solution)/shard_map/pallas_call | solution.py:325
  25.0 18.5 %all_to_all.10 = f32[32,16,128]{2,1,0:T(8,128)S(1)} all-to-all(f32[32,16,128]{2,1,0:T(8,128)S(1)} %get-tuple-element.11), channel_id=1, replica_groups=mesh['wide'=32,'narrow'=4] {'wide'}, dimensions={0} | all-to-all | bytes 524288 | tf_op jit(solution)/shard_map/all_to_all | solution.py:436
  43.6 3.1 %collective-permute-start.2 = (f32[16,128]{1,0:T(8,128)S(1)}, f32[16,128]{1,0:T(8,128)S(1)}, u32[]{:S(2)}, u32[]{:S(2)}) collective-permute-start(f32[16,128]{1,0:T(8,128)S(1)} %reduce_sum.9.own_ref), channel_id=1, source_target_pairs={{0,3},{1,0},{2,1},{3,2},{4,7},{5,4},{6,5},{7,6},{8,11},{9,8},{10,9... | collective-permute-start | bytes 24584 | tf_op jit(solution)/shard_map/ppermute | solution.py:438
  46.7 0.9 %collective-permute-start.1 = (f32[16,128]{1,0:T(8,128)S(1)}, f32[16,128]{1,0:T(8,128)S(1)}, u32[]{:S(2)}, u32[]{:S(2)}) collective-permute-start(f32[16,128]{1,0:T(8,128)S(1)} %reduce_sum.9.own_ref), channel_id=1, source_target_pairs={{0,2},{1,3},{2,0},{3,1},{4,6},{5,7},{6,4},{7,5},{8,10},{9,11},{10,... | collective-permute-start | bytes 24584 | tf_op jit(solution)/shard_map/ppermute | solution.py:438
  47.6 0.0 collective-permute-start
  47.6 0.0 copy-start
  47.6 2.2 %shard_map.140.inv_ref = f32[1,1024,1024]{2,1,0:T(8,128)S(1)} custom-call(f32[16,128]{1,0:T(8,128)S(1)} %reduce_sum.9.own_ref, f32[1,1024,1024]{2,1,0:T(8,128)} %inv_hbm.1), custom_call_target="tpu_custom_call" | custom-call | bytes 8388608 | tf_op jit(solution)/shard_map/pallas_call | solution.py:440
  49.9 0.0 collective-permute-done.2.three_ref
  49.9 0.8 %collective-permute-done.1.two_ref = f32[16,128]{1,0:T(8,128)S(1)} collective-permute-done((f32[16,128]{1,0:T(8,128)S(1)}, f32[16,128]{1,0:T(8,128)S(1)}, u32[]{:S(2)}, u32[]{:S(2)}) %collective-permute-start.1) | collective-permute-done | bytes 8224 | tf_op jit(solution)/shard_map/ppermute | solution.py:438
  50.7 0.9 %collective-permute-done.one_ref = f32[16,128]{1,0:T(8,128)S(1)} collective-permute-done((f32[16,128]{1,0:T(8,128)S(1)}, f32[16,128]{1,0:T(8,128)S(1)}, u32[]{:S(2)}, u32[]{:S(2)}) %collective-permute-start) | collective-permute-done | bytes 8224 | tf_op jit(solution)/shard_map/ppermute | solution.py:438
  51.6 0.0 copy-done
  51.6 1.6 %shard_map.141 = (f32[32,8,128]{2,1,0:T(8,128)}, f32[4,256]{1,0:T(4,128)S(1)}, f32[4,256]{1,0:T(4,128)S(1)}) custom-call(s32[1]{0:T(128)} %bitcast.7.group_ref, f32[16,128]{1,0:T(8,128)S(1)} %reduce_sum.9.own_ref, f32[16,128]{1,0:T(8,128)S(1)} %collective-permute-done.one_ref, f32[16,128]{1,0:T(8,128)S(1)} %collective-permute-done.1.two_ref, ...), custom_call_target="tpu_custom_call" | custom-call | tf_op jit(solution)/shard_map/pallas_call | solution.py:453
  53.3 5.1 %all-to-all-start.1 = ((f32[32,8,128]{2,1,0:T(8,128)}), f32[32,8,128]{2,1,0:T(8,128)S(1)}, u32[]{:S(2)}, u32[]{:S(2)}) async-start(f32[32,8,128]{2,1,0:T(8,128)} %get-tuple-element.12), calls=%async_computation.1 | async-start | bytes 262144 | tf_op jit(solution)/shard_map/all_to_all | solution.py:462
  58.4 7.8 %all-to-all-done.1.recv_ref = f32[32,8,128]{2,1,0:T(8,128)S(1)} async-done(((f32[32,8,128]{2,1,0:T(8,128)}), f32[32,8,128]{2,1,0:T(8,128)S(1)}, u32[]{:S(2)}, u32[]{:S(2)}) %all-to-all-start.1) | async-done | bytes 131104 | tf_op jit(solution)/shard_map/all_to_all | solution.py:462
  66.2 0.7 %shard_map.142 = (f32[4,256]{1,0:T(4,128)}, f32[3,504]{1,0:T(4,128)}) custom-call(s32[1]{0:T(128)} %bitcast.6.mine_ref, f32[32,8,128]{2,1,0:T(8,128)S(1)} %all-to-all-done.1.recv_ref, f32[4,256]{1,0:T(4,128)S(1)} %get-tuple-element.13.mul_ref, f32[4,256]{1,0:T(4,128)S(1)} %get-tuple-element.14.add_ref), custom_call_target="tpu_custom_call" | custom-call | tf_op jit(solution)/shard_map/pallas_call | solution.py:464
  (1 shorter events, 0.0 us)
Async XLA Ops:
  43.6 6.3 %collective-permute-start.2 = (f32[16,128]{1,0:T(8,128)S(1)}, f32[16,128]{1,0:T(8,128)S(1)}, u32[]{:S(2)}, u32[]{:S(2)}) collective-permute-start(f32[16,128]{1,0:T(8,128)S(1)} %reduce_sum.9.own_ref), channel_id=1, source_target_pairs={{0,3},{1,0},{2,1},{3,2},{4,7},{5,4},{6,5},{7,6},{8,11},{9,8},{10,9... | collective-permute-start | bytes 24584 | tf_op jit(solution)/shard_map/ppermute | solution.py:438
  46.7 4.0 %collective-permute-start.1 = (f32[16,128]{1,0:T(8,128)S(1)}, f32[16,128]{1,0:T(8,128)S(1)}, u32[]{:S(2)}, u32[]{:S(2)}) collective-permute-start(f32[16,128]{1,0:T(8,128)S(1)} %reduce_sum.9.own_ref), channel_id=1, source_target_pairs={{0,2},{1,3},{2,0},{3,1},{4,6},{5,7},{6,4},{7,5},{8,10},{9,11},{10,... | collective-permute-start | bytes 24584 | tf_op jit(solution)/shard_map/ppermute | solution.py:438
  47.6 4.0 %collective-permute-start = (f32[16,128]{1,0:T(8,128)S(1)}, f32[16,128]{1,0:T(8,128)S(1)}, u32[]{:S(2)}, u32[]{:S(2)}) collective-permute-start(f32[16,128]{1,0:T(8,128)S(1)} %reduce_sum.9.own_ref), channel_id=1, source_target_pairs={{0,1},{1,2},{2,3},{3,0},{4,5},{5,6},{6,7},{7,4},{8,9},{9,10},{10,1... | collective-permute-start | bytes 24584 | tf_op jit(solution)/shard_map/ppermute | solution.py:438
  47.6 4.0 %copy-start = (f32[4,256]{1,0:T(4,128)S(1)}, f32[4,256]{1,0:T(4,128)}, u32[]{:S(2)}) copy-start(f32[4,256]{1,0:T(4,128)} %decay_ref.1) | copy-start | bytes 12292
  53.3 12.9 %all-to-all-start.1 = ((f32[32,8,128]{2,1,0:T(8,128)}), f32[32,8,128]{2,1,0:T(8,128)S(1)}, u32[]{:S(2)}, u32[]{:S(2)}) async-start(f32[32,8,128]{2,1,0:T(8,128)} %get-tuple-element.12), calls=%async_computation.1 | async-start | bytes 262144 | tf_op jit(solution)/shard_map/all_to_all | solution.py:462
